TPU v7x, 32 devices: a whole 2x2x4 slice. The times are simulated.
32 devices in a mesh: groups: 2 (over y), tm: 8 (over z, core), chan: 2 (over x), rows: 1.
Axes of the slice: x: 2, y: 2, z: 4, core: 2. Of those that a mesh axis runs over, the one named last changes fastest.
Arguments:
- video: bfloat16 [32, 8, 32, 512], P(('groups', 'tm'), 'rows', None, 'chan'), parts along dimension 0, may hold values from -6 to 6
- channel_gain: float32 [512], P('chan'), may hold values from 0.1 to 1.9
- weights: bfloat16 [27, 512, 512], P(None, None, 'chan'), may hold values from -0.0546875 to 0.0546875
- lengths: int32 [8], P('groups'), parts along dimension 0, may hold values from 1 to 8, 16 in all
- cotangent: bfloat16 [32, 8, 32, 512], P(('groups', 'tm'), 'rows', None, 'chan'), parts along dimension 0, may hold values from -6 to 6
Outputs:
- output: bfloat16 [32, 8, 32, 512], P(('groups', 'tm'), 'rows', None, 'chan'), parts along dimension 0
- input_grad: bfloat16 [32, 8, 32, 512], P(('groups', 'tm'), 'rows', None, 'chan'), parts along dimension 0
- weight_grad: float32 [54, 512, 512], P('groups', ('tm', 'rows'), 'chan'), parts along dimension 0
There are 2 independent parts, one for each index of `groups`. A program takes and returns all parts, laid end to end along the dimension named above; an argument that names none is the same for every part. Nothing has to cross between parts.
Inputs may be any that keep to these rules, and one draw needn't show every extreme that they name: The 4 lengths sum to 16; the longest is exactly 8.
All inputs are finite; a program needn't handle non-finite values.
Results may differ from a plain program's by a relative error of at most 0.004.
Values may be sent and summed in bfloat16 or wider, within the bound.
No kernel may reach another device: no remote copies, remote signals or barrier semaphores. Data moves between devices by JAX's collectives and lax.ppermute only.
A program may use at most 128 MiB of HBM per device.

v0:
```python
import functools, math
import jax, jax.numpy as jnp
from jax import lax
from jax.experimental import pallas as pl
from jax.experimental.pallas import tpu as pltpu
from jax.sharding import PartitionSpec as P


LAGS = 3
SIDE = 3


def first_of(lens, count, frame):
    start, first = jnp.int32(0), jnp.int32(0)
    for i in range(count):
        first = jnp.where(start <= frame, start, first)
        start = start + lens[i]
    return first


def opens(lens, count, frame):
    start, hit = jnp.int32(0), jnp.int32(0)
    for i in range(count):
        hit = jnp.where(start == frame, 1, hit)
        start = start + lens[i]
    return hit


def joined(lens, count, frame, later):
    end, cut = jnp.int32(0), jnp.int32(0)
    for i in range(count):
        end = end + lens[i]
        cut = jnp.where((frame < end) & (end <= later), 1, cut)
    return 1 - cut


def moved(value, steps, width):
    rows = value.shape[0]
    col = lax.broadcasted_iota(jnp.int32, value.shape, 0) % width
    if steps == 1:
        return jnp.where(col == width - 1, 0.0, pltpu.roll(value, rows - 1, 0))
    return jnp.where(col == 0, 0.0, pltpu.roll(value, 1, 0))


def silu_body(video, gain, out):
    scaled = video[...].astype(jnp.float32) * gain[...]
    out[...] = (scaled / (1.0 + jnp.exp(-scaled))).astype(out.dtype)


def silu(video, gain):
    whole = pl.BlockSpec(memory_space=pltpu.VMEM)
    return pl.pallas_call(
        silu_body,
        out_shape=jax.ShapeDtypeStruct(video.shape, video.dtype),
        in_specs=[whole, whole],
        out_specs=whole,
        cost_estimate=pl.CostEstimate(flops=8 * video.size, transcendentals=video.size, bytes_accessed=4 * video.size),
        name="silu",
    )(video, gain.reshape(1, -1))


def forward_body(parts, clips, where_ref, lens, video, *refs):
    own, past = refs[:parts], refs[parts : 2 * parts]
    weights, out, padded, acc = refs[2 * parts :]
    frames, rows, width, chans = video.shape
    step = pl.program_id(0)
    base, chan = where_ref[0], where_ref[1]

    @pl.when(step == 0)
    def _():
        edge = jnp.zeros((2 * frames, 1, width, chans), padded.dtype)
        for j in range(parts):
            padded[j, :, 0:1] = edge
            padded[j, :, rows + 1 : rows + 2] = edge
            padded[j, 0:frames, 1 : rows + 1] = past[j][...]
            padded[j, frames : 2 * frames, 1 : rows + 1] = own[j][...]
        acc[...] = jnp.zeros_like(acc)

    lag, row_step = step // SIDE, step % SIDE
    for j in range(parts):
        shard = lax.rem(chan + j, parts)
        taps = []
        for f in range(frames):
            frame = base + f
            source = jnp.maximum(frame - lag, first_of(lens, clips, frame)) - base + frames
            taps.append(padded[j, source, pl.ds(row_step, rows)].reshape(rows * width, chans))
        taps = jnp.concatenate(taps, axis=0)
        for b in range(SIDE):
            kernel = weights[b, pl.ds(pl.multiple_of(shard * chans, chans), chans), :]
            acc[b] += jnp.dot(taps, kernel, preferred_element_type=jnp.float32)

    @pl.when(step == LAGS * SIDE - 1)
    def _():
        total = acc[1] + moved(acc[0], -1, width) + moved(acc[2], 1, width)
        out[...] = (video[...].astype(jnp.float32) + total.reshape(video.shape)).astype(out.dtype)


def forward(where, lens, video, own, past, weights):
    frames, rows, width, chans = video.shape
    parts, pixels = len(own), frames * rows * width
    whole = pl.BlockSpec(memory_space=pltpu.VMEM)
    smem = pl.BlockSpec(memory_space=pltpu.SMEM)
    flops = 2 * pixels * weights.shape[0] * weights.shape[1] * weights.shape[2]
    return pl.pallas_call(
        functools.partial(forward_body, parts, lens.shape[0]),
        grid=(LAGS * SIDE,),
        out_shape=jax.ShapeDtypeStruct(video.shape, video.dtype),
        in_specs=[smem, smem, whole] + [whole] * (2 * parts)
        + [pl.BlockSpec((SIDE,) + weights.shape[1:], lambda i: (i, 0, 0))],
        out_specs=whole,
        scratch_shapes=[
            pltpu.VMEM((parts, 2 * frames, rows + 2, width, chans), video.dtype),
            pltpu.VMEM((SIDE, pixels, weights.shape[2]), jnp.float32),
        ],
        compiler_params=pltpu.CompilerParams(vmem_limit_bytes=24 << 20),
        cost_estimate=pl.CostEstimate(flops=flops, transcendentals=0, bytes_accessed=2 * weights.size),
        name="forward",
    )(where, lens, video, *own, *past, weights)


def backward_body(parts, clips, where_ref, lens, own, later, weights, mine, *refs):
    others, (mixed, acc) = refs[: parts - 1], refs[parts - 1 :]
    frames, rows, width, chans = own.shape
    step = pl.program_id(0)
    base, chan = where_ref[0], where_ref[1]

    @pl.when(step == 0)
    def _():
        mixed[:, :, 0:1] = jnp.zeros((LAGS, frames, 1, width, chans), mixed.dtype)
        mixed[:, :, rows + 1 : rows + 2] = jnp.zeros((LAGS, frames, 1, width, chans), mixed.dtype)
        take = lambda f: (own[f] if f < frames else later[f - frames]).astype(jnp.float32)
        for f in range(frames):
            frame = base + f
            start = opens(lens, clips, frame).astype(jnp.float32)
            next_one = joined(lens, clips, frame, frame + 1).astype(jnp.float32)
            next_two = joined(lens, clips, frame, frame + 2).astype(jnp.float32)
            mixed[0, f, 1 : rows + 1] = own[f]
            mixed[1, f, 1 : rows + 1] = (next_one * take(f + 1) + start * take(f)).astype(mixed.dtype)
            mixed[2, f, 1 : rows + 1] = (
                next_two * take(f + 2) + start * (take(f) + next_one * take(f + 1))
            ).astype(mixed.dtype)
        acc[...] = jnp.zeros_like(acc)

    lag, row_step = step // SIDE, step % SIDE
    taps = mixed[lag, :, pl.ds(2 - row_step, rows)].reshape(frames * rows * width, chans)
    for j in range(parts):
        shard = lax.rem(chan + j, parts)
        for b in range(SIDE):
            kernel = weights[b, pl.ds(pl.multiple_of(shard * chans, chans), chans), :]
            acc[j, b] += lax.dot_general(
                taps, kernel, (((1,), (1,)), ((), ())), preferred_element_type=jnp.float32
            )

    @pl.when(step == LAGS * SIDE - 1)
    def _():
        for j in range(parts):
            total = acc[j, 1] + moved(acc[j, 0], 1, width) + moved(acc[j, 2], -1, width)
            if j == 0:
                mine[...] = total.reshape(mine.shape)
            else:
                others[j - 1][...] = total.reshape(mine.shape).astype(others[j - 1].dtype)


def backward(where, lens, own, later, weights):
    frames, rows, width, chans = own.shape
    parts, pixels = weights.shape[1] // chans, frames * rows * width
    whole = pl.BlockSpec(memory_space=pltpu.VMEM)
    smem = pl.BlockSpec(memory_space=pltpu.SMEM)
    flops = 2 * pixels * weights.shape[0] * weights.shape[1] * weights.shape[2]
    return pl.pallas_call(
        functools.partial(backward_body, parts, lens.shape[0]),
        grid=(LAGS * SIDE,),
        out_shape=[jax.ShapeDtypeStruct(own.shape, jnp.float32)]
        + [jax.ShapeDtypeStruct(own.shape, own.dtype)] * (parts - 1),
        in_specs=[smem, smem, whole, whole, pl.BlockSpec((SIDE,) + weights.shape[1:], lambda i: (i, 0, 0))],
        out_specs=[whole] * parts,
        scratch_shapes=[
            pltpu.VMEM((LAGS, frames, rows + 2, width, chans), own.dtype),
            pltpu.VMEM((parts, SIDE, pixels, chans), jnp.float32),
        ],
        compiler_params=pltpu.CompilerParams(vmem_limit_bytes=24 << 20),
        cost_estimate=pl.CostEstimate(flops=flops, transcendentals=0, bytes_accessed=2 * weights.size),
        name="backward",
    )(where, lens, own, later, weights)


def turned_body(parts, where_ref, *refs):
    own, outs, rows = refs[:parts], refs[parts:-1], refs[-1]
    chans = own[0].shape[1]
    for j in range(parts):
        shard = lax.rem(where_ref[1] + j, parts)
        rows[pl.ds(pl.multiple_of(shard * chans, chans), chans), :] = own[j][...].T
    pair = where_ref[2] // 2
    for offset, out in enumerate(outs):
        size = out.shape[0]
        out[...] = rows[pl.ds(pl.multiple_of((pair ^ offset) * size, size), size), :]


def turned(where, own, pairs):
    pixels, chans = own[0].shape
    all_chans = len(own) * chans
    whole = pl.BlockSpec(memory_space=pltpu.VMEM)
    return pl.pallas_call(
        functools.partial(turned_body, len(own)),
        out_shape=[jax.ShapeDtypeStruct((all_chans // pairs, pixels), own[0].dtype)] * pairs,
        in_specs=[pl.BlockSpec(memory_space=pltpu.SMEM)] + [whole] * len(own),
        out_specs=[whole] * pairs,
        scratch_shapes=[pltpu.VMEM((all_chans, pixels), own[0].dtype)],
        cost_estimate=pl.CostEstimate(flops=pixels * chans * 64, transcendentals=0, bytes_accessed=4 * pixels * chans),
        name="turned",
    )(where, *own)


def weight_body(blocks, frames, rows, width, clips, scale, where_ref, lens, *refs):
    turned_refs, cots, (out, taps) = refs[:blocks], refs[blocks : 2 * blocks], refs[2 * blocks :]
    chans, pixels = out.shape[1], turned_refs[0].shape[1]
    area = rows * width
    shard = where_ref[2]

    place = lax.broadcasted_iota(jnp.int32, (1, pixels), 1)
    row, col = (place % area) // width, place % width
    masks = {}
    for a in range(SIDE):
        for b in range(SIDE):
            r, c = row + a - 1, col + b - 1
            masks[a, b] = ((r >= 0) & (r < rows) & (c >= 0) & (c < width)).astype(jnp.float32)

    lane = pl.ds(pl.multiple_of((shard % 2) * chans, chans), chans)
    for offset in range(blocks):
        block = shard ^ offset
        value = turned_refs[offset][lane, :].astype(jnp.float32)
        for a in range(SIDE):
            for b in range(SIDE):
                step = (a - 1) * width + b - 1
                copy = value if step == 0 else pltpu.roll(value, (-step) % pixels, 1) * masks[a, b]
                copy = copy.astype(taps.dtype)
                at = (SIDE * a + b) * chans
                for f in range(frames):
                    taps[block * frames + f, at : at + chans] = copy[:, f * area : (f + 1) * area]
    for offset in range(blocks):
        first = (shard ^ offset) * frames

        def lagged(lag, carry, offset=offset, first=first):
            pieces = []
            for f in range(frames):
                frame = first + f
                source = jnp.maximum(frame - lag, first_of(lens, clips, frame))
                pieces.append(taps[source])
            terms = jnp.dot(jnp.concatenate(pieces, axis=1), cots[offset][...], preferred_element_type=jnp.float32)
            at = pl.ds(lag * SIDE * SIDE, SIDE * SIDE)
            terms = terms.reshape(SIDE * SIDE, chans, terms.shape[1])
            if offset == 0:
                out[at] = terms
            elif offset == blocks - 1:
                out[at] = (out[at] + terms) * scale
            else:
                out[at] += terms
            return carry

        lax.fori_loop(0, LAGS, lagged, 0)


def weight_terms(where, lens, turned_blocks, cots, rows, width, scale):
    blocks, pixels = len(cots), cots[0].shape[0]
    chans = turned_blocks[0].shape[0] // 2
    area = rows * width
    frames = pixels // area
    outs = cots[0].shape[1]
    whole = pl.BlockSpec(memory_space=pltpu.VMEM)
    smem = pl.BlockSpec(memory_space=pltpu.SMEM)
    taps = SIDE * SIDE
    return pl.pallas_call(
        functools.partial(weight_body, blocks, frames, rows, width, lens.shape[0], scale),
        out_shape=jax.ShapeDtypeStruct((LAGS * taps, chans, outs), jnp.float32),
        in_specs=[smem, smem] + [whole] * (2 * blocks),
        out_specs=whole,
        scratch_shapes=[pltpu.VMEM((blocks * frames, taps * chans, area), turned_blocks[0].dtype)],
        compiler_params=pltpu.CompilerParams(vmem_limit_bytes=28 << 20),
        cost_estimate=pl.CostEstimate(
            flops=2 * blocks * pixels * LAGS * taps * chans * outs, transcendentals=0, bytes_accessed=8 << 20),
        name="weight_terms",
    )(where, lens, *turned_blocks, *cots)


def extended_2(cells, sides, width):
    for axis, dim in sides:
        count = lax.axis_size(axis)
        ends = count - 1
        head = lax.slice_in_dim(cells, 0, width, axis=dim)
        tail = lax.slice_in_dim(cells, cells.shape[dim] - width, cells.shape[dim], axis=dim)
        cells = jnp.concatenate(
            [
                lax.ppermute(tail, axis, [(i, (i + 1) % count) for i in range(ends)]),
                cells,
                lax.ppermute(head, axis, [((i + 1) % count, i) for i in range(ends)]),
            ],
            axis=dim,
        )
    return cells


def shifted(value, axis, steps):
    count = lax.axis_size(axis)
    leading, last = (max(0, -steps), min(count, count - steps))
    return lax.ppermute(value, axis, [(source, source + steps) for source in range(leading, last)])


def clip_tables(lengths, frame_ids):
    clip_ends = jnp.cumsum(lengths)
    clip_starts = clip_ends - lengths
    clip_ids = jnp.sum((frame_ids[:, None] >= clip_ends[None, :]).astype(jnp.int32), axis=1)
    clip_first = jnp.max(
        jnp.where(clip_starts[None, :] <= frame_ids[:, None], clip_starts[None, :], 0), axis=1
    )
    opening = jnp.any(clip_starts[None, :] == frame_ids[:, None], axis=1)
    return (clip_ids, clip_first, opening)


def input_terms(grad_frames, weights, row_count, col_count):
    frame_total = grad_frames.shape[0]
    local_chans = grad_frames.shape[3]
    all_chans = weights.shape[1]
    pieces = []
    for lag_step in range(3):
        back_stack = jnp.stack(
            [
                grad_frames[
                    :,
                    2 - row_step : 2 - row_step + row_count,
                    2 - col_step : 2 - col_step + col_count,
                    :,
                ]
                for row_step in range(3)
                for col_step in range(3)
            ],
            axis=3,
        ).reshape(frame_total * row_count * col_count, 9 * local_chans)
        back_kernel = jnp.transpose(weights[9 * lag_step : 9 * lag_step + 9], (0, 2, 1)).reshape(
            9 * local_chans, all_chans
        )
        pieces.append(
            jnp.dot(back_stack, back_kernel, preferred_element_type=jnp.float32).reshape(
                frame_total, row_count, col_count, all_chans
            )
        )
    return pieces


def lag_mix(lagged, clip_ids, opening, frame_count):
    here_ids = clip_ids[:frame_count]
    start_flag = opening[:frame_count].astype(jnp.float32)
    act_grad = jnp.zeros((frame_count,) + lagged[0].shape[1:], jnp.float32)
    for lag_step in range(3):
        same_clip = (clip_ids[lag_step : lag_step + frame_count] == here_ids).astype(jnp.float32)
        act_grad = (
            act_grad
            + same_clip[:, None, None, None] * lagged[lag_step][lag_step : lag_step + frame_count]
        )
        for inner_step in range(lag_step):
            near_clip = (clip_ids[inner_step : inner_step + frame_count] == here_ids).astype(
                jnp.float32
            ) * start_flag
            act_grad = (
                act_grad
                + near_clip[:, None, None, None]
                * lagged[lag_step][inner_step : inner_step + frame_count]
            )
    return act_grad


def split_rows(video, channel_gain, weights, lengths, cotangent):
    frame_count, row_count, col_count, local_chans = video.shape
    all_chans = weights.shape[1]
    pixel_count = frame_count * row_count * col_count
    total_pixels = pixel_count * lax.axis_size("tm") * lax.axis_size("rows")
    frame_base = lax.axis_index("tm") * frame_count
    frame_ids = frame_base + jnp.arange(frame_count + 2, dtype=jnp.int32)
    clip_ids, clip_first, opening = clip_tables(lengths, frame_ids)
    own_frames = frame_ids[:frame_count]
    scaled = video.astype(jnp.float32) * channel_gain
    activated = jax.nn.silu(scaled).astype(jnp.bfloat16)
    paired = extended_2(jnp.stack([activated, cotangent]), (("rows", 2),), 1)
    paired = jnp.pad(paired, ((0, 0), (0, 0), (0, 0), (1, 1), (0, 0)))
    act_pad = paired[0]
    grad_pad = paired[1]
    prior_rows = shifted(act_pad, "tm", 1)
    extended = jnp.concatenate([prior_rows, act_pad], axis=0)
    gathered = lax.all_gather(extended, "chan", axis=3, tiled=True)
    flat_grad = cotangent.reshape(pixel_count, local_chans)
    output_sum = jnp.zeros((pixel_count, local_chans), jnp.float32)
    weight_terms = []
    for lag_step in range(3):
        distance = jnp.minimum(lag_step, own_frames - clip_first[:frame_count])[:, None, None, None]
        chosen = jnp.where(
            distance == 0,
            gathered[2 : frame_count + 2],
            jnp.where(distance == 1, gathered[1 : frame_count + 1], gathered[0:frame_count]),
        )
        tap_stack = jnp.stack(
            [
                chosen[:, row_step : row_step + row_count, col_step : col_step + col_count, :]
                for row_step in range(3)
                for col_step in range(3)
            ],
            axis=3,
        ).reshape(pixel_count, 9 * all_chans)
        kernel = weights[9 * lag_step : 9 * lag_step + 9].reshape(9 * all_chans, local_chans)
        output_sum = output_sum + jnp.dot(tap_stack, kernel, preferred_element_type=jnp.float32)
        weight_terms.append(
            lax.dot_general(
                tap_stack, flat_grad, (((0,), (0,)), ((), ())), preferred_element_type=jnp.float32
            ).reshape(9, all_chans, local_chans)
        )
    output = (
        video.astype(jnp.float32)
        + output_sum.reshape(frame_count, row_count, col_count, local_chans)
    ).astype(jnp.bfloat16)
    own_terms = lax.psum_scatter(
        jnp.stack(input_terms(grad_pad, weights, row_count, col_count)),
        "chan",
        scatter_dimension=4,
        tiled=True,
    )
    arriving = shifted(
        jnp.concatenate([own_terms[1, 0:1], own_terms[2, 0:2]], axis=0).astype(jnp.bfloat16),
        "tm",
        -1,
    ).astype(jnp.float32)
    lagged = [
        own_terms[0],
        jnp.concatenate([own_terms[1], arriving[0:1]], axis=0),
        jnp.concatenate([own_terms[2], arriving[1:3]], axis=0),
    ]
    act_grad = lag_mix(lagged, clip_ids, opening, frame_count)
    sigmoid_value = jax.nn.sigmoid(scaled)
    slope_factor = sigmoid_value * (1.0 + scaled * (1.0 - sigmoid_value))
    input_grad = (cotangent.astype(jnp.float32) + act_grad * slope_factor * channel_gain).astype(
        jnp.bfloat16
    )
    weight_sum = jnp.concatenate(weight_terms, axis=0)
    summed = lax.psum_scatter(weight_sum, ("tm", "rows"), scatter_dimension=1, tiled=True)
    weight_grad = summed * (1.0 / math.sqrt(total_pixels))
    return (output, input_grad, weight_grad)


def along(value, axis, steps):
    count = lax.axis_size(axis)
    first, last = max(0, -steps), min(count, count - steps)
    return lax.ppermute(value, axis, [(source, source + steps) for source in range(first, last)])


def across(value, axis, offset):
    return lax.ppermute(value, axis, [(i, i ^ offset) for i in range(lax.axis_size(axis))])


def ahead(value, axis, steps):
    count = lax.axis_size(axis)
    return lax.ppermute(value, axis, [((i + steps) % count, i) for i in range(count)])


def gathered_blocks(own, axis):
    blocks = {0: own}
    bit = lax.axis_size(axis) // 2
    while bit:
        for offset in list(blocks):
            blocks[offset ^ bit] = across(blocks[offset], axis, bit)
        bit //= 2
    return [blocks[offset] for offset in range(len(blocks))]


def whole_rows(video, channel_gain, weights, lengths, cotangent):
    frames, rows, width, chans = video.shape
    all_chans = weights.shape[1]
    parts, shards = all_chans // chans, lax.axis_size("tm")
    pixels = frames * rows * width
    weights = pltpu.with_memory_space_constraint(weights, pltpu.HBM)
    shard, chan = lax.axis_index("tm"), lax.axis_index("chan")
    where = jnp.stack([shard * frames, chan, shard]).astype(jnp.int32)
    scaled = video.astype(jnp.float32) * channel_gain
    activated = silu(video.reshape(pixels, chans), channel_gain).reshape(video.shape)
    own = [activated] + [ahead(activated, "chan", j) for j in range(1, parts)]
    before = along(activated, "tm", 1)
    past = [before] + [ahead(before, "chan", j) for j in range(1, parts)]
    later = along(cotangent, "tm", -1)
    cots = gathered_blocks(cotangent.reshape(pixels, chans), "tm")
    mine, *others = backward(where, lengths, cotangent, later, weights)
    act_grad = mine
    for j in range(1, parts):
        act_grad = act_grad + ahead(others[j - 1], "chan", parts - j).astype(jnp.float32)
    sent = turned(where, [x.reshape(pixels, chans) for x in own], shards // 2)
    blocks = []
    for offset in range(shards // 2):
        block = across(sent[offset], "tm", 2 * offset) if offset else sent[0]
        blocks += [block, across(block, "tm", 1)]
    output = forward(where, lengths, video, own, past, weights)
    sigmoid_value = jax.nn.sigmoid(scaled)
    slope_factor = sigmoid_value * (1.0 + scaled * (1.0 - sigmoid_value))
    input_grad = (cotangent.astype(jnp.float32) + act_grad * slope_factor * channel_gain).astype(jnp.bfloat16)
    scale = 1.0 / math.sqrt(pixels * shards)
    weight_grad = weight_terms(where, lengths, blocks, cots, rows, width, scale)
    return (output, input_grad, weight_grad)


def solution(mesh):
    in_specs = (
        P(("groups", "tm"), "rows", None, "chan"),
        P("chan"),
        P(None, None, "chan"),
        P("groups"),
        P(("groups", "tm"), "rows", None, "chan"),
    )
    out_specs = (
        P(("groups", "tm"), "rows", None, "chan"),
        P(("groups", "tm"), "rows", None, "chan"),
        P("groups", ("tm", "rows"), "chan"),
    )
    body = whole_rows if mesh.shape["rows"] == 1 else split_rows
    return jax.shard_map(body, mesh=mesh, in_specs=in_specs, out_specs=out_specs, check_vma=False)
```

profile of v0, /device:TPU:0, one launch (start us, length us, event | category | flops | bytes accessed | tf_op | source)
XLA Modules:
  0.0 65.5 jit_solution(1006016748789626994)
XLA Ops:
  0.6 1.8 %silu.1.refs_0_ = bf16[512,256]{1,0:T(8,128)(2,1)} custom-call(bf16[512,256]{1,0:T(8,128)(2,1)} %bitcast.11, f32[1,256]{1,0:T(1,128)} %bitcast.17), custom_call_target="tpu_custom_call" | custom-call | flops 1048576 | bytes 524288 | tf_op jit(solution)/shard_map/silu/pallas_call | solution.py:52
  2.4 3.0 %collective-permute-start = (bf16[2,8,32,256]{3,2,1,0:T(8,128)(2,1)}, bf16[2,8,32,256]{3,2,1,0:T(8,128)(2,1)S(1)}, u32[]{:S(2)}, u32[]{:S(2)}) collective-permute-start(bf16[2,8,32,256]{3,2,1,0:T(8,128)(2,1)} %bitcast.8), channel_id=1, source_target_pairs={{1,0},{0,1},{3,2},{2,3},{5,4},{4,5},{7,6},{6,7},{9,8},{8,9},{11,10... | collective-permute-start | bytes 786440 | tf_op jit(solution)/shard_map/ppermute | solution.py:458
  5.4 1.5 %collective-permute-start.1 = (bf16[2,8,32,256]{3,2,1,0:T(8,128)(2,1)}, bf16[2,8,32,256]{3,2,1,0:T(8,128)(2,1)S(1)}, u32[]{:S(2)}, u32[]{:S(2)}) collective-permute-start(bf16[2,8,32,256]{3,2,1,0:T(8,128)(2,1)} %bitcast.9), channel_id=1, source_target_pairs={{0,2},{2,4},{4,6},{6,8},{8,10},{10,12},{12,14},{1,3},{3,5},{5,7},{... | collective-permute-start | bytes 786440 | tf_op jit(solution)/shard_map/ppermute | solution.py:449
  6.9 3.1 %collective-permute-start.15 = (bf16[512,256]{1,0:T(8,128)(2,1)}, bf16[512,256]{1,0:T(8,128)(2,1)S(1)}, u32[]{:S(2)}, u32[]{:S(2)}) collective-permute-start(bf16[512,256]{1,0:T(8,128)(2,1)} %bitcast.13), channel_id=1, source_target_pairs={{0,8},{2,10},{4,12},{6,14},{8,0},{10,2},{12,4},{14,6},{1,9},{3,11}... | collective-permute-start | bytes 786440 | tf_op jit(solution)/shard_map/ppermute | solution.py:453
  10.0 1.3 %collective-permute-start.3 = (bf16[2,8,32,256]{3,2,1,0:T(8,128)(2,1)}, bf16[2,8,32,256]{3,2,1,0:T(8,128)(2,1)S(1)}, u32[]{:S(2)}, u32[]{:S(2)}) collective-permute-start(bf16[2,8,32,256]{3,2,1,0:T(8,128)(2,1)} %own.1), channel_id=1, source_target_pairs={{2,0},{4,2},{6,4},{8,6},{10,8},{12,10},{14,12},{3,1},{5,3},{7,5},{... | collective-permute-start | bytes 786440 | tf_op jit(solution)/shard_map/ppermute | solution.py:449
  11.3 3.7 %collective-permute-start.13 = (bf16[512,256]{1,0:T(8,128)(2,1)}, bf16[512,256]{1,0:T(8,128)(2,1)S(1)}, u32[]{:S(2)}, u32[]{:S(2)}) collective-permute-start(bf16[512,256]{1,0:T(8,128)(2,1)} %bitcast.14), channel_id=1, source_target_pairs={{0,4},{2,6},{4,0},{6,2},{8,12},{10,14},{12,8},{14,10},{1,5},{3,7},... | collective-permute-start | bytes 786440 | tf_op jit(solution)/shard_map/ppermute | solution.py:453
  15.0 0.6 pad_add_fusion.where_ref
  15.6 0.0 collective-permute-done.refs_1_
  15.6 0.0 collective-permute-start.12
  15.6 0.7 %copy-done.2 = bf16[2,8,32,256]{3,2,1,0:T(8,128)(2,1)} copy-done((bf16[2,8,32,256]{3,2,1,0:T(8,128)(2,1)}, bf16[2,8,32,256]{3,2,1,0:T(8,128)(2,1)S(1)}, u32[]{:S(2)}) %copy-start.2) | copy-done | bytes 262168
  16.3 2.0 %turned.1 = (bf16[128,512]{1,0:T(8,128)(2,1)}, bf16[128,512]{1,0:T(8,128)(2,1)}, bf16[128,512]{1,0:T(8,128)(2,1)}, bf16[128,512]{1,0:T(8,128)(2,1)}) custom-call(s32[3]{0:T(128)} %pad_add_fusion.where_ref, bf16[512,256]{1,0:T(8,128)(2,1)} %silu.1.refs_0_, bf16[512,256]{1,0:T(8,128)(2,1)} %bitcast.12), custom_call_target="tpu_custom_call" | custom-call | flops 8388608 | bytes 524288 | tf_op jit(solution)/shard_map/turned/pallas_call | solution.py:203
  18.4 0.0 collective-permute-done.1.refs_2_
  18.4 0.1 collective-permute-start.6
  18.4 3.6 %collective-permute-done.15.refs_12_ = bf16[512,256]{1,0:T(8,128)(2,1)S(1)} collective-permute-done((bf16[512,256]{1,0:T(8,128)(2,1)}, bf16[512,256]{1,0:T(8,128)(2,1)S(1)}, u32[]{:S(2)}, u32[]{:S(2)}) %collective-permute-start.15) | collective-permute-done | bytes 262176 | tf_op jit(solution)/shard_map/ppermute | solution.py:453
  22.0 0.7 %collective-permute-start.8 = (bf16[128,512]{1,0:T(8,128)(2,1)}, bf16[128,512]{1,0:T(8,128)(2,1)S(1)}, u32[]{:S(2)}, u32[]{:S(2)}) collective-permute-start(bf16[128,512]{1,0:T(8,128)(2,1)} %get-tuple-element.13), channel_id=1, source_target_pairs={{0,8},{2,10},{4,12},{6,14},{8,0},{10,2},{12,4},{14,6},{1,9},{3,11}... | collective-permute-start | bytes 393224 | tf_op jit(solution)/shard_map/ppermute | solution.py:453
  22.7 0.0 collective-permute-done.3.later
  22.7 0.5 collective-permute-start.2
  23.2 0.9 %copy-done.4 = bf16[2,8,32,256]{3,2,1,0:T(8,128)(2,1)S(1)} copy-done((bf16[2,8,32,256]{3,2,1,0:T(8,128)(2,1)S(1)}, bf16[2,8,32,256]{3,2,1,0:T(8,128)(2,1)}, u32[]{:S(2)}) %copy-start.4) | copy-done | bytes 262168
  24.2 0.7 %copy-done.6 = s32[3]{0:T(128)S(1)} copy-done((s32[3]{0:T(128)S(1)}, s32[3]{0:T(128)}, u32[]{:S(2)}) %copy-start.6) | copy-done | bytes 36
  24.9 0.7 copy-done.9
  25.5 9.7 %backward.1 = (f32[2,8,32,256]{3,2,1,0:T(8,128)S(1)}, bf16[2,8,32,256]{3,2,1,0:T(8,128)(2,1)S(1)}) custom-call(s32[3]{0:T(128)S(1)} %copy-done.6, s32[4]{0:T(128)S(1)} %copy-done.9, bf16[2,8,32,256]{3,2,1,0:T(8,128)(2,1)S(1)} %copy-done.4, bf16[2,8,32,256]{3,2,1,0:T(8,128)(2,1)S(1)} %collective-permute-done.3.later, bf16[27,512,256]{2,1,0:T(8,128)(2,1)} %weights.1), custom_call_target="tpu_custom_call" | custom-call | flops 3623878656 | bytes 7077888 | tf_op jit(solution)/shard_map/backward/pallas_call | solution.py:170
  35.2 0.0 copy-start.11
  35.2 0.0 collective-permute-done.13.refs_10_
  35.2 4.3 %collective-permute-start.10 = (bf16[128,512]{1,0:T(8,128)(2,1)S(1)}, bf16[128,512]{1,0:T(8,128)(2,1)S(1)}, u32[]{:S(2)}, u32[]{:S(2)}) collective-permute-start(bf16[128,512]{1,0:T(8,128)(2,1)S(1)} %copy-done.12), channel_id=1, source_target_pairs={{0,12},{2,14},{4,8},{6,10},{8,4},{10,6},{12,0},{14,2},{1,13},{3,15... | collective-permute-start | bytes 393224 | tf_op jit(solution)/shard_map/ppermute | solution.py:453
  39.5 0.0 collective-permute-done.12.refs_9_
  39.5 0.4 collective-permute-start.5
  40.0 0.0 collective-permute-done.6.refs_2_
  40.0 1.6 %collective-permute-start.4 = (bf16[2,8,32,256]{3,2,1,0:T(8,128)(2,1)S(1)}, bf16[2,8,32,256]{3,2,1,0:T(8,128)(2,1)S(1)}, u32[]{:S(2)}, u32[]{:S(2)}) collective-permute-start(bf16[2,8,32,256]{3,2,1,0:T(8,128)(2,1)S(1)} %get-tuple-element.10), channel_id=1, source_target_pairs={{1,0},{0,1},{3,2},{2,3},{5,4},{4,5},{7,6},{6,7},{9,8},{8,9},{11,10... | collective-permute-start | bytes 786440 | tf_op jit(solution)/shard_map/ppermute | solution.py:458
  41.5 0.0 collective-permute-done.8.refs_4_
  41.6 0.7 collective-permute-start.17
  42.2 0.0 collective-permute-done.2.refs_3_
  42.2 0.0 collective-permute-start.7
  42.2 9.8 %forward.1 = bf16[2,8,32,256]{3,2,1,0:T(8,128)(2,1)} custom-call(s32[3]{0:T(128)S(1)} %copy-done.6, s32[4]{0:T(128)S(1)} %copy-done.9, bf16[2,8,32,256]{3,2,1,0:T(8,128)(2,1)S(1)} %copy-done.1, bf16[2,8,32,256]{3,2,1,0:T(8,128)(2,1)S(1)} %bitcast.10, bf16[2,8,32,256]{3,2,1,0:T(8,128)(2,1)S(1)} %copy-done.3, ...), custom_call_target="tpu_custom_call" | custom-call | flops 3623878656 | bytes 7077888 | tf_op jit(solution)/shard_map/forward/pallas_call | solution.py:104
  52.1 0.0 collective-permute-done.10.refs_6_
  52.1 0.5 collective-permute-start.16
  52.5 0.0 collective-permute-done.5.refs_1_
  52.5 0.1 collective-permute-start.14
  52.6 0.0 collective-permute-done.7.refs_3_
  52.6 0.4 collective-permute-start.9
  53.1 0.0 collective-permute-done.17.refs_14_
  53.1 0.1 collective-permute-start.11
  53.1 0.0 collective-permute-done.4
  53.1 0.4 collective-permute-start.18
  53.6 1.0 %add_convert_fusion = bf16[2,8,32,256]{3,2,1,0:T(8,128)(2,1)} fusion(bf16[2,8,32,256]{3,2,1,0:T(8,128)(2,1)S(1)} %copy-done.1, f32[2,8,32,256]{3,2,1,0:T(8,128)S(1)} %get-tuple-element.9, bf16[2,8,32,256]{3,2,1,0:T(8,128)(2,1)S(1)} %collective-permute-done.4, bf16[2,8,32,256]{3,2,1,0:T(8,128)(2,1)S(1)} %copy-done.4, f32[256]{0:T(256)S(1)} %copy-done.11), kind=kLoop, calls=%fused_computation | loop fusion | flops 2097152 | bytes 1573888 | tf_op jit(solution)/shard_map/convert_element_type | solution.py:498
  54.6 0.0 collective-permute-done.9.refs_5_
  54.6 0.0 collective-permute-done.14.refs_11_
  54.6 0.2 collective-permute-done.18.refs_15_
  54.8 10.7 %weight_terms.1 = f32[27,64,256]{2,1,0:T(8,128)} custom-call(s32[3]{0:T(128)S(1)} %copy-done.7, s32[4]{0:T(128)S(1)} %copy-done.10, bf16[128,512]{1,0:T(8,128)(2,1)S(1)} %copy-done.8, bf16[128,512]{1,0:T(8,128)(2,1)S(1)} %collective-permute-done.5.refs_1_, bf16[128,512]{1,0:T(8,128)(2,1)S(1)} %collective-permute-done.6.refs_2_, ...), custom_call_target="tpu_custom_call" | custom-call | flops 3623878656 | bytes 8388608 | tf_op jit(solution)/shard_map/weight_terms/pallas_call | solution.py:272
  (23 shorter events, 0.0 us)
Async XLA Ops:
  2.4 39.8 %copy-start = (bf16[512,256]{1,0:T(8,128)(2,1)S(1)}, bf16[512,256]{1,0:T(8,128)(2,1)}, u32[]{:S(2)}) copy-start(bf16[512,256]{1,0:T(8,128)(2,1)} %silu.1.refs_0_) | copy-start | bytes 786436
  2.4 39.8 %copy-start.1 = (bf16[2,8,32,256]{3,2,1,0:T(8,128)(2,1)S(1)}, bf16[2,8,32,256]{3,2,1,0:T(8,128)(2,1)}, u32[]{:S(2)}) copy-start(bf16[2,8,32,256]{3,2,1,0:T(8,128)(2,1)} %video.1) | copy-start | bytes 786436
  2.4 13.2 %collective-permute-start = (bf16[2,8,32,256]{3,2,1,0:T(8,128)(2,1)}, bf16[2,8,32,256]{3,2,1,0:T(8,128)(2,1)S(1)}, u32[]{:S(2)}, u32[]{:S(2)}) collective-permute-start(bf16[2,8,32,256]{3,2,1,0:T(8,128)(2,1)} %bitcast.8), channel_id=1, source_target_pairs={{1,0},{0,1},{3,2},{2,3},{5,4},{4,5},{7,6},{6,7},{9,8},{8,9},{11,10... | collective-permute-start | bytes 786440 | tf_op jit(solution)/shard_map/ppermute | solution.py:458
  5.4 12.9 %collective-permute-start.1 = (bf16[2,8,32,256]{3,2,1,0:T(8,128)(2,1)}, bf16[2,8,32,256]{3,2,1,0:T(8,128)(2,1)S(1)}, u32[]{:S(2)}, u32[]{:S(2)}) collective-permute-start(bf16[2,8,32,256]{3,2,1,0:T(8,128)(2,1)} %bitcast.9), channel_id=1, source_target_pairs={{0,2},{2,4},{4,6},{6,8},{8,10},{10,12},{12,14},{1,3},{3,5},{5,7},{... | collective-permute-start | bytes 786440 | tf_op jit(solution)/shard_map/ppermute | solution.py:449
  6.9 15.2 %collective-permute-start.15 = (bf16[512,256]{1,0:T(8,128)(2,1)}, bf16[512,256]{1,0:T(8,128)(2,1)S(1)}, u32[]{:S(2)}, u32[]{:S(2)}) collective-permute-start(bf16[512,256]{1,0:T(8,128)(2,1)} %bitcast.13), channel_id=1, source_target_pairs={{0,8},{2,10},{4,12},{6,14},{8,0},{10,2},{12,4},{14,6},{1,9},{3,11}... | collective-permute-start | bytes 786440 | tf_op jit(solution)/shard_map/ppermute | solution.py:453
  10.0 12.7 %collective-permute-start.3 = (bf16[2,8,32,256]{3,2,1,0:T(8,128)(2,1)}, bf16[2,8,32,256]{3,2,1,0:T(8,128)(2,1)S(1)}, u32[]{:S(2)}, u32[]{:S(2)}) collective-permute-start(bf16[2,8,32,256]{3,2,1,0:T(8,128)(2,1)} %own.1), channel_id=1, source_target_pairs={{2,0},{4,2},{6,4},{8,6},{10,8},{12,10},{14,12},{3,1},{5,3},{7,5},{... | collective-permute-start | bytes 786440 | tf_op jit(solution)/shard_map/ppermute | solution.py:449
  11.3 23.9 %collective-permute-start.13 = (bf16[512,256]{1,0:T(8,128)(2,1)}, bf16[512,256]{1,0:T(8,128)(2,1)S(1)}, u32[]{:S(2)}, u32[]{:S(2)}) collective-permute-start(bf16[512,256]{1,0:T(8,128)(2,1)} %bitcast.14), channel_id=1, source_target_pairs={{0,4},{2,6},{4,0},{6,2},{8,12},{10,14},{12,8},{14,10},{1,5},{3,7},... | collective-permute-start | bytes 786440 | tf_op jit(solution)/shard_map/ppermute | solution.py:453
  15.6 0.7 %copy-start.2 = (bf16[2,8,32,256]{3,2,1,0:T(8,128)(2,1)}, bf16[2,8,32,256]{3,2,1,0:T(8,128)(2,1)S(1)}, u32[]{:S(2)}) copy-start(bf16[2,8,32,256]{3,2,1,0:T(8,128)(2,1)S(1)} %collective-permute-done.refs_1_) | copy-start | bytes 786436
  15.6 23.9 %collective-permute-start.12 = (bf16[512,256]{1,0:T(8,128)(2,1)}, bf16[512,256]{1,0:T(8,128)(2,1)S(1)}, u32[]{:S(2)}, u32[]{:S(2)}) collective-permute-start(bf16[512,256]{1,0:T(8,128)(2,1)} %bitcast.15), channel_id=1, source_target_pairs={{0,2},{2,0},{4,6},{6,4},{8,10},{10,8},{12,14},{14,12},{1,3},{3,1},... | collective-permute-start | bytes 786440 | tf_op jit(solution)/shard_map/ppermute | solution.py:453
  18.4 23.9 %copy-start.3 = (bf16[2,8,32,256]{3,2,1,0:T(8,128)(2,1)S(1)}, bf16[2,8,32,256]{3,2,1,0:T(8,128)(2,1)}, u32[]{:S(2)}) copy-start(bf16[2,8,32,256]{3,2,1,0:T(8,128)(2,1)} %copy-done.2) | copy-start | bytes 786436
  18.4 21.6 %collective-permute-start.6 = (bf16[128,512]{1,0:T(8,128)(2,1)}, bf16[128,512]{1,0:T(8,128)(2,1)S(1)}, u32[]{:S(2)}, u32[]{:S(2)}) collective-permute-start(bf16[128,512]{1,0:T(8,128)(2,1)} %get-tuple-element.12), channel_id=1, source_target_pairs={{0,4},{2,6},{4,0},{6,2},{8,12},{10,14},{12,8},{14,10},{1,5},{3,7},... | collective-permute-start | bytes 393224 | tf_op jit(solution)/shard_map/ppermute | solution.py:453
  22.0 19.5 %collective-permute-start.8 = (bf16[128,512]{1,0:T(8,128)(2,1)}, bf16[128,512]{1,0:T(8,128)(2,1)S(1)}, u32[]{:S(2)}, u32[]{:S(2)}) collective-permute-start(bf16[128,512]{1,0:T(8,128)(2,1)} %get-tuple-element.13), channel_id=1, source_target_pairs={{0,8},{2,10},{4,12},{6,14},{8,0},{10,2},{12,4},{14,6},{1,9},{3,11}... | collective-permute-start | bytes 393224 | tf_op jit(solution)/shard_map/ppermute | solution.py:453
  22.7 19.5 %collective-permute-start.2 = (bf16[2,8,32,256]{3,2,1,0:T(8,128)(2,1)S(1)}, bf16[2,8,32,256]{3,2,1,0:T(8,128)(2,1)S(1)}, u32[]{:S(2)}, u32[]{:S(2)}) collective-permute-start(bf16[2,8,32,256]{3,2,1,0:T(8,128)(2,1)S(1)} %collective-permute-done.1.refs_2_), channel_id=1, source_target_pairs={{1,0},{0,1},{3,2},{2,3},{5,4},{4,5},{7,6},{6,7},{9,8},{8,9},{11,10... | collective-permute-start | bytes 786440 | tf_op jit(solution)/shard_map/ppermute | solution.py:458
  23.2 0.9 %copy-start.4 = (bf16[2,8,32,256]{3,2,1,0:T(8,128)(2,1)S(1)}, bf16[2,8,32,256]{3,2,1,0:T(8,128)(2,1)}, u32[]{:S(2)}) copy-start(bf16[2,8,32,256]{3,2,1,0:T(8,128)(2,1)} %own.1) | copy-start | bytes 786436
  24.2 0.7 %copy-start.6 = (s32[3]{0:T(128)S(1)}, s32[3]{0:T(128)}, u32[]{:S(2)}) copy-start(s32[3]{0:T(128)} %pad_add_fusion.where_ref) | copy-start | bytes 40
  24.8 0.7 %copy-start.9 = (s32[4]{0:T(128)S(1)}, s32[4]{0:T(128)}, u32[]{:S(2)}) copy-start(s32[4]{0:T(128)} %lens.5) | copy-start | bytes 52
  25.5 9.7 %copy-start.12 = (bf16[128,512]{1,0:T(8,128)(2,1)S(1)}, bf16[128,512]{1,0:T(8,128)(2,1)}, u32[]{:S(2)}) copy-start(bf16[128,512]{1,0:T(8,128)(2,1)} %get-tuple-element.14) | copy-start | bytes 393220
  25.5 14.0 %copy-start.8 = (bf16[128,512]{1,0:T(8,128)(2,1)S(1)}, bf16[128,512]{1,0:T(8,128)(2,1)}, u32[]{:S(2)}) copy-start(bf16[128,512]{1,0:T(8,128)(2,1)} %get-tuple-element.11.refs_0_) | copy-start | bytes 393220
  35.2 18.4 %copy-start.11 = (f32[256]{0:T(256)S(1)}, f32[256]{0:T(256)}, u32[]{:S(2)}) copy-start(f32[256]{0:T(256)} %param.6) | copy-start | bytes 3076
  35.2 16.9 %collective-permute-start.10 = (bf16[128,512]{1,0:T(8,128)(2,1)S(1)}, bf16[128,512]{1,0:T(8,128)(2,1)S(1)}, u32[]{:S(2)}, u32[]{:S(2)}) collective-permute-start(bf16[128,512]{1,0:T(8,128)(2,1)S(1)} %copy-done.12), channel_id=1, source_target_pairs={{0,12},{2,14},{4,8},{6,10},{8,4},{10,6},{12,0},{14,2},{1,13},{3,15... | collective-permute-start | bytes 393224 | tf_op jit(solution)/shard_map/ppermute | solution.py:453
  39.5 13.0 %collective-permute-start.5 = (bf16[128,512]{1,0:T(8,128)(2,1)S(1)}, bf16[128,512]{1,0:T(8,128)(2,1)S(1)}, u32[]{:S(2)}, u32[]{:S(2)}) collective-permute-start(bf16[128,512]{1,0:T(8,128)(2,1)S(1)} %copy-done.8), channel_id=1, source_target_pairs={{0,2},{2,0},{4,6},{6,4},{8,10},{10,8},{12,14},{14,12},{1,3},{3,1},... | collective-permute-start | bytes 393224 | tf_op jit(solution)/shard_map/ppermute | solution.py:453
  40.0 14.9 %copy-start.5 = (bf16[2,8,32,256]{3,2,1,0:T(8,128)(2,1)S(1)}, bf16[2,8,32,256]{3,2,1,0:T(8,128)(2,1)}, u32[]{:S(2)}) copy-start(bf16[2,8,32,256]{3,2,1,0:T(8,128)(2,1)} %own.1) | copy-start | bytes 786436
  40.0 14.9 %copy-start.7 = (s32[3]{0:T(128)S(1)}, s32[3]{0:T(128)}, u32[]{:S(2)}) copy-start(s32[3]{0:T(128)} %pad_add_fusion.where_ref) | copy-start | bytes 40
  40.0 14.9 %copy-start.10 = (s32[4]{0:T(128)S(1)}, s32[4]{0:T(128)}, u32[]{:S(2)}) copy-start(s32[4]{0:T(128)} %lens.5) | copy-start | bytes 52
  40.0 13.2 %collective-permute-start.4 = (bf16[2,8,32,256]{3,2,1,0:T(8,128)(2,1)S(1)}, bf16[2,8,32,256]{3,2,1,0:T(8,128)(2,1)S(1)}, u32[]{:S(2)}, u32[]{:S(2)}) collective-permute-start(bf16[2,8,32,256]{3,2,1,0:T(8,128)(2,1)S(1)} %get-tuple-element.10), channel_id=1, source_target_pairs={{1,0},{0,1},{3,2},{2,3},{5,4},{4,5},{7,6},{6,7},{9,8},{8,9},{11,10... | collective-permute-start | bytes 786440 | tf_op jit(solution)/shard_map/ppermute | solution.py:458
  41.6 11.5 %collective-permute-start.17 = (bf16[512,256]{1,0:T(8,128)(2,1)S(1)}, bf16[512,256]{1,0:T(8,128)(2,1)S(1)}, u32[]{:S(2)}, u32[]{:S(2)}) collective-permute-start(bf16[512,256]{1,0:T(8,128)(2,1)S(1)} %collective-permute-done.15.refs_12_), channel_id=1, source_target_pairs={{0,4},{2,6},{4,0},{6,2},{8,12},{10,14},{12,8},{14,10},{1,5},{3,7},... | collective-permute-start | bytes 786440 | tf_op jit(solution)/shard_map/ppermute | solution.py:453
  42.2 10.4 %collective-permute-start.7 = (bf16[128,512]{1,0:T(8,128)(2,1)S(1)}, bf16[128,512]{1,0:T(8,128)(2,1)S(1)}, u32[]{:S(2)}, u32[]{:S(2)}) collective-permute-start(bf16[128,512]{1,0:T(8,128)(2,1)S(1)} %collective-permute-done.6.refs_2_), channel_id=1, source_target_pairs={{0,2},{2,0},{4,6},{6,4},{8,10},{10,8},{12,14},{14,12},{1,3},{3,1},... | collective-permute-start | bytes 393224 | tf_op jit(solution)/shard_map/ppermute | solution.py:453
  52.1 2.5 %collective-permute-start.16 = (bf16[512,256]{1,0:T(8,128)(2,1)S(1)}, bf16[512,256]{1,0:T(8,128)(2,1)S(1)}, u32[]{:S(2)}, u32[]{:S(2)}) collective-permute-start(bf16[512,256]{1,0:T(8,128)(2,1)S(1)} %collective-permute-done.15.refs_12_), channel_id=1, source_target_pairs={{0,2},{2,0},{4,6},{6,4},{8,10},{10,8},{12,14},{14,12},{1,3},{3,1},... | collective-permute-start | bytes 786440 | tf_op jit(solution)/shard_map/ppermute | solution.py:453
  52.5 2.1 %collective-permute-start.14 = (bf16[512,256]{1,0:T(8,128)(2,1)S(1)}, bf16[512,256]{1,0:T(8,128)(2,1)S(1)}, u32[]{:S(2)}, u32[]{:S(2)}) collective-permute-start(bf16[512,256]{1,0:T(8,128)(2,1)S(1)} %collective-permute-done.13.refs_10_), channel_id=1, source_target_pairs={{0,2},{2,0},{4,6},{6,4},{8,10},{10,8},{12,14},{14,12},{1,3},{3,1},... | collective-permute-start | bytes 786440 | tf_op jit(solution)/shard_map/ppermute | solution.py:453
  52.6 2.0 %collective-permute-start.9 = (bf16[128,512]{1,0:T(8,128)(2,1)S(1)}, bf16[128,512]{1,0:T(8,128)(2,1)S(1)}, u32[]{:S(2)}, u32[]{:S(2)}) collective-permute-start(bf16[128,512]{1,0:T(8,128)(2,1)S(1)} %collective-permute-done.8.refs_4_), channel_id=1, source_target_pairs={{0,2},{2,0},{4,6},{6,4},{8,10},{10,8},{12,14},{14,12},{1,3},{3,1},... | collective-permute-start | bytes 393224 | tf_op jit(solution)/shard_map/ppermute | solution.py:453
  53.1 1.5 %collective-permute-start.11 = (bf16[128,512]{1,0:T(8,128)(2,1)S(1)}, bf16[128,512]{1,0:T(8,128)(2,1)S(1)}, u32[]{:S(2)}, u32[]{:S(2)}) collective-permute-start(bf16[128,512]{1,0:T(8,128)(2,1)S(1)} %collective-permute-done.10.refs_6_), channel_id=1, source_target_pairs={{0,2},{2,0},{4,6},{6,4},{8,10},{10,8},{12,14},{14,12},{1,3},{3,1},... | collective-permute-start | bytes 393224 | tf_op jit(solution)/shard_map/ppermute | solution.py:453
  53.1 1.7 %collective-permute-start.18 = (bf16[512,256]{1,0:T(8,128)(2,1)S(1)}, bf16[512,256]{1,0:T(8,128)(2,1)S(1)}, u32[]{:S(2)}, u32[]{:S(2)}) collective-permute-start(bf16[512,256]{1,0:T(8,128)(2,1)S(1)} %collective-permute-done.17.refs_14_), channel_id=1, source_target_pairs={{0,2},{2,0},{4,6},{6,4},{8,10},{10,8},{12,14},{14,12},{1,3},{3,1},... | collective-permute-start | bytes 786440 | tf_op jit(solution)/shard_map/ppermute | solution.py:453
where the time goes:
time: 66 us; the launch traced here: 65.5 us
  Pallas kernels  34 us (52%)
  starting transfers between devices  22.3 us (34%)
  waiting for transfers between devices  3.85 us (6%)
  local copies, waits for them, and re-layouts  3 us (5%)
  other arithmetic  1.66 us (3%)
  between operations  0.75 us (1%)
    ppermute x14, starting transfers between devices, across(): lax.ppermute(value, axis, [(i, i ^ offset) for i in range(lax.axis_size(a...  14.5 us
    pallas_call x1, Pallas kernels, weight_terms(): pl.pallas_call(functools.partial(weight_body, blocks, frames, rows, width...  10.7 us
    pallas_call x1, Pallas kernels, forward(): pl.pallas_call(functools.partial(forward_body, parts, lens.shape[0]), gri...  9.82 us
    pallas_call x1, Pallas kernels, backward(): pl.pallas_call(functools.partial(backward_body, parts, lens.shape[0]), gr...  9.65 us
    ppermute x3, starting transfers between devices, ahead(): lax.ppermute(value, axis, [((i + steps) % count, i) for i in range(count)])  5.06 us
    ppermute x14, waiting for transfers between devices, across(): lax.ppermute(value, axis, [(i, i ^ offset) for i in range(lax.axis_size(a...  3.84 us
    unnamed x26, local copies, waits for them, and re-layouts  3 us
    ppermute x2, starting transfers between devices, along(): lax.ppermute(value, axis, [(source, source + steps) for source in range(f...  2.74 us
  transfers between devices with their start and end apart: 19, of which 2 were waited for; matrix products, arithmetic and copies ran while one was open for 3% of the time, Pallas kernels for 33%

commit v1 on v0

--- a/solution.py
+++ b/solution.py
@@ -8,6 +8,7 @@
 
 LAGS = 3
 SIDE = 3
+PLACES = 3
 
 
 def first_of(lens, count, frame):
@@ -54,134 +55,151 @@
         out_shape=jax.ShapeDtypeStruct(video.shape, video.dtype),
         in_specs=[whole, whole],
         out_specs=whole,
+        compiler_params=pltpu.CompilerParams(vmem_limit_bytes=4 << 20),
         cost_estimate=pl.CostEstimate(flops=8 * video.size, transcendentals=video.size, bytes_accessed=4 * video.size),
         name="silu",
     )(video, gain.reshape(1, -1))
 
 
-def forward_body(parts, clips, where_ref, lens, video, *refs):
+def fetch(weights, held, sems):
+    for row_step in range(SIDE):
+        for lag in range(LAGS):
+            for b in range(SIDE):
+                tap = SIDE * (SIDE * lag + row_step) + b
+                pltpu.make_async_copy(weights.at[tap], held.at[tap], sems.at[tap]).start()
+
+
+def arrived(weights, held, sems, row_step):
+    for lag in range(LAGS):
+        for b in range(SIDE):
+            tap = SIDE * (SIDE * lag + row_step) + b
+            pltpu.make_async_copy(weights.at[tap], held.at[tap], sems.at[tap]).wait()
+
+
+def forward_body(parts, clips, where_ref, video, *refs):
     own, past = refs[:parts], refs[parts : 2 * parts]
-    weights, out, padded, acc = refs[2 * parts :]
+    weights, out, padded, acc, held, sems = refs[2 * parts :]
     frames, rows, width, chans = video.shape
-    step = pl.program_id(0)
     base, chan = where_ref[0], where_ref[1]
-
-    @pl.when(step == 0)
-    def _():
-        edge = jnp.zeros((2 * frames, 1, width, chans), padded.dtype)
-        for j in range(parts):
-            padded[j, :, 0:1] = edge
-            padded[j, :, rows + 1 : rows + 2] = edge
-            padded[j, 0:frames, 1 : rows + 1] = past[j][...]
-            padded[j, frames : 2 * frames, 1 : rows + 1] = own[j][...]
-        acc[...] = jnp.zeros_like(acc)
-
-    lag, row_step = step // SIDE, step % SIDE
+    lens = [where_ref[PLACES + i] for i in range(clips)]
+    fetch(weights, held, sems)
+    edge = jnp.zeros((2 * frames, 1, width, chans), padded.dtype)
     for j in range(parts):
         shard = lax.rem(chan + j, parts)
+        padded[shard, :, 0:1] = edge
+        padded[shard, :, rows + 1 : rows + 2] = edge
+        padded[shard, 0:frames, 1 : rows + 1] = past[j][...]
+        padded[shard, frames : 2 * frames, 1 : rows + 1] = own[j][...]
+    acc[...] = jnp.zeros_like(acc)
+
+    def step(row_step, carry):
+        arrived(weights, held, sems, row_step)
         taps = []
         for f in range(frames):
             frame = base + f
-            source = jnp.maximum(frame - lag, first_of(lens, clips, frame)) - base + frames
-            taps.append(padded[j, source, pl.ds(row_step, rows)].reshape(rows * width, chans))
+            pieces = []
+            for lag in range(LAGS):
+                source = jnp.maximum(frame - lag, first_of(lens, clips, frame)) - base + frames
+                for j in range(parts):
+                    pieces.append(padded[j, source, pl.ds(row_step, rows)].reshape(rows * width, chans))
+            taps.append(jnp.concatenate(pieces, axis=1))
         taps = jnp.concatenate(taps, axis=0)
         for b in range(SIDE):
-            kernel = weights[b, pl.ds(pl.multiple_of(shard * chans, chans), chans), :]
+            kernel = jnp.concatenate([held[SIDE * (SIDE * lag + row_step) + b] for lag in range(LAGS)], axis=0)
             acc[b] += jnp.dot(taps, kernel, preferred_element_type=jnp.float32)
-
-    @pl.when(step == LAGS * SIDE - 1)
-    def _():
-        total = acc[1] + moved(acc[0], -1, width) + moved(acc[2], 1, width)
-        out[...] = (video[...].astype(jnp.float32) + total.reshape(video.shape)).astype(out.dtype)
-
-
-def forward(where, lens, video, own, past, weights):
+        return carry
+
+    lax.fori_loop(0, SIDE, step, 0)
+    total = acc[1] + moved(acc[0], -1, width) + moved(acc[2], 1, width)
+    out[...] = (video[...].astype(jnp.float32) + total.reshape(video.shape)).astype(out.dtype)
+
+
+def forward(where, video, own, past, weights):
     frames, rows, width, chans = video.shape
     parts, pixels = len(own), frames * rows * width
     whole = pl.BlockSpec(memory_space=pltpu.VMEM)
     smem = pl.BlockSpec(memory_space=pltpu.SMEM)
-    flops = 2 * pixels * weights.shape[0] * weights.shape[1] * weights.shape[2]
     return pl.pallas_call(
-        functools.partial(forward_body, parts, lens.shape[0]),
-        grid=(LAGS * SIDE,),
+        functools.partial(forward_body, parts, where.shape[0] - PLACES),
         out_shape=jax.ShapeDtypeStruct(video.shape, video.dtype),
-        in_specs=[smem, smem, whole] + [whole] * (2 * parts)
-        + [pl.BlockSpec((SIDE,) + weights.shape[1:], lambda i: (i, 0, 0))],
+        in_specs=[smem, whole] + [whole] * (2 * parts) + [pl.BlockSpec(memory_space=pltpu.HBM)],
         out_specs=whole,
         scratch_shapes=[
             pltpu.VMEM((parts, 2 * frames, rows + 2, width, chans), video.dtype),
             pltpu.VMEM((SIDE, pixels, weights.shape[2]), jnp.float32),
+            pltpu.VMEM(weights.shape, weights.dtype),
+            pltpu.SemaphoreType.DMA((weights.shape[0],)),
         ],
-        compiler_params=pltpu.CompilerParams(vmem_limit_bytes=24 << 20),
-        cost_estimate=pl.CostEstimate(flops=flops, transcendentals=0, bytes_accessed=2 * weights.size),
+        compiler_params=pltpu.CompilerParams(vmem_limit_bytes=20 << 20),
+        cost_estimate=pl.CostEstimate(
+            flops=2 * pixels * weights.size, transcendentals=0, bytes_accessed=2 * weights.size),
         name="forward",
-    )(where, lens, video, *own, *past, weights)
-
-
-def backward_body(parts, clips, where_ref, lens, own, later, weights, mine, *refs):
-    others, (mixed, acc) = refs[: parts - 1], refs[parts - 1 :]
+    )(where, video, *own, *past, weights)
+
+
+def backward_body(parts, clips, where_ref, own, later, weights, mine, *refs):
+    others, (mixed, acc, held, sems) = refs[: parts - 1], refs[parts - 1 :]
     frames, rows, width, chans = own.shape
-    step = pl.program_id(0)
+    pixels = frames * rows * width
     base, chan = where_ref[0], where_ref[1]
-
-    @pl.when(step == 0)
-    def _():
-        mixed[:, :, 0:1] = jnp.zeros((LAGS, frames, 1, width, chans), mixed.dtype)
-        mixed[:, :, rows + 1 : rows + 2] = jnp.zeros((LAGS, frames, 1, width, chans), mixed.dtype)
-        take = lambda f: (own[f] if f < frames else later[f - frames]).astype(jnp.float32)
-        for f in range(frames):
-            frame = base + f
-            start = opens(lens, clips, frame).astype(jnp.float32)
-            next_one = joined(lens, clips, frame, frame + 1).astype(jnp.float32)
-            next_two = joined(lens, clips, frame, frame + 2).astype(jnp.float32)
-            mixed[0, f, 1 : rows + 1] = own[f]
-            mixed[1, f, 1 : rows + 1] = (next_one * take(f + 1) + start * take(f)).astype(mixed.dtype)
-            mixed[2, f, 1 : rows + 1] = (
-                next_two * take(f + 2) + start * (take(f) + next_one * take(f + 1))
-            ).astype(mixed.dtype)
-        acc[...] = jnp.zeros_like(acc)
-
-    lag, row_step = step // SIDE, step % SIDE
-    taps = mixed[lag, :, pl.ds(2 - row_step, rows)].reshape(frames * rows * width, chans)
+    lens = [where_ref[PLACES + i] for i in range(clips)]
+    fetch(weights, held, sems)
+    mixed[:, :, 0:1] = jnp.zeros((LAGS, frames, 1, width, chans), mixed.dtype)
+    mixed[:, :, rows + 1 : rows + 2] = jnp.zeros((LAGS, frames, 1, width, chans), mixed.dtype)
+    take = lambda f: (own[f] if f < frames else later[f - frames]).astype(jnp.float32)
+    for f in range(frames):
+        frame = base + f
+        start = opens(lens, clips, frame).astype(jnp.float32)
+        next_one = joined(lens, clips, frame, frame + 1).astype(jnp.float32)
+        next_two = joined(lens, clips, frame, frame + 2).astype(jnp.float32)
+        mixed[0, f, 1 : rows + 1] = own[f]
+        mixed[1, f, 1 : rows + 1] = (next_one * take(f + 1) + start * take(f)).astype(mixed.dtype)
+        mixed[2, f, 1 : rows + 1] = (
+            next_two * take(f + 2) + start * (take(f) + next_one * take(f + 1))
+        ).astype(mixed.dtype)
+    acc[...] = jnp.zeros_like(acc)
+
+    def step(row_step, carry):
+        arrived(weights, held, sems, row_step)
+        taps = [mixed[lag, :, pl.ds(2 - row_step, rows)].reshape(pixels, chans) for lag in range(LAGS)]
+        taps = jnp.concatenate(taps, axis=1)
+        for b in range(SIDE):
+            kernel = jnp.concatenate([held[SIDE * (SIDE * lag + row_step) + b] for lag in range(LAGS)], axis=1)
+            acc[b] += lax.dot_general(taps, kernel, (((1,), (1,)), ((), ())), preferred_element_type=jnp.float32)
+        return carry
+
+    lax.fori_loop(0, SIDE, step, 0)
     for j in range(parts):
-        shard = lax.rem(chan + j, parts)
-        for b in range(SIDE):
-            kernel = weights[b, pl.ds(pl.multiple_of(shard * chans, chans), chans), :]
-            acc[j, b] += lax.dot_general(
-                taps, kernel, (((1,), (1,)), ((), ())), preferred_element_type=jnp.float32
-            )
-
-    @pl.when(step == LAGS * SIDE - 1)
-    def _():
-        for j in range(parts):
-            total = acc[j, 1] + moved(acc[j, 0], 1, width) + moved(acc[j, 2], -1, width)
-            if j == 0:
-                mine[...] = total.reshape(mine.shape)
-            else:
-                others[j - 1][...] = total.reshape(mine.shape).astype(others[j - 1].dtype)
-
-
-def backward(where, lens, own, later, weights):
+        at = pl.ds(pl.multiple_of(lax.rem(chan + j, parts) * chans, chans), chans)
+        total = acc[1, :, at] + moved(acc[0, :, at], 1, width) + moved(acc[2, :, at], -1, width)
+        if j == 0:
+            mine[...] = total.reshape(mine.shape)
+        else:
+            others[j - 1][...] = total.reshape(mine.shape).astype(others[j - 1].dtype)
+
+
+def backward(where, own, later, weights):
     frames, rows, width, chans = own.shape
     parts, pixels = weights.shape[1] // chans, frames * rows * width
     whole = pl.BlockSpec(memory_space=pltpu.VMEM)
     smem = pl.BlockSpec(memory_space=pltpu.SMEM)
-    flops = 2 * pixels * weights.shape[0] * weights.shape[1] * weights.shape[2]
     return pl.pallas_call(
-        functools.partial(backward_body, parts, lens.shape[0]),
-        grid=(LAGS * SIDE,),
+        functools.partial(backward_body, parts, where.shape[0] - PLACES),
         out_shape=[jax.ShapeDtypeStruct(own.shape, jnp.float32)]
         + [jax.ShapeDtypeStruct(own.shape, own.dtype)] * (parts - 1),
-        in_specs=[smem, smem, whole, whole, pl.BlockSpec((SIDE,) + weights.shape[1:], lambda i: (i, 0, 0))],
+        in_specs=[smem, whole, whole, pl.BlockSpec(memory_space=pltpu.HBM)],
         out_specs=[whole] * parts,
         scratch_shapes=[
             pltpu.VMEM((LAGS, frames, rows + 2, width, chans), own.dtype),
-            pltpu.VMEM((parts, SIDE, pixels, chans), jnp.float32),
+            pltpu.VMEM((SIDE, pixels, parts * chans), jnp.float32),
+            pltpu.VMEM(weights.shape, weights.dtype),
+            pltpu.SemaphoreType.DMA((weights.shape[0],)),
         ],
-        compiler_params=pltpu.CompilerParams(vmem_limit_bytes=24 << 20),
-        cost_estimate=pl.CostEstimate(flops=flops, transcendentals=0, bytes_accessed=2 * weights.size),
+        compiler_params=pltpu.CompilerParams(vmem_limit_bytes=20 << 20),
+        cost_estimate=pl.CostEstimate(
+            flops=2 * pixels * weights.size, transcendentals=0, bytes_accessed=2 * weights.size),
         name="backward",
-    )(where, lens, own, later, weights)
+    )(where, own, later, weights)
 
 
 def turned_body(parts, where_ref, *refs):
@@ -206,80 +224,80 @@
         in_specs=[pl.BlockSpec(memory_space=pltpu.SMEM)] + [whole] * len(own),
         out_specs=[whole] * pairs,
         scratch_shapes=[pltpu.VMEM((all_chans, pixels), own[0].dtype)],
+        compiler_params=pltpu.CompilerParams(vmem_limit_bytes=4 << 20),
         cost_estimate=pl.CostEstimate(flops=pixels * chans * 64, transcendentals=0, bytes_accessed=4 * pixels * chans),
         name="turned",
     )(where, *own)
 
 
-def weight_body(blocks, frames, rows, width, clips, scale, where_ref, lens, *refs):
+def weight_body(blocks, group, rows, width, clips, scale, where_ref, *refs):
     turned_refs, cots, (out, taps) = refs[:blocks], refs[blocks : 2 * blocks], refs[2 * blocks :]
-    chans, pixels = out.shape[1], turned_refs[0].shape[1]
-    area = rows * width
+    pixels = turned_refs[0].shape[1]
+    area, chans, outs = rows * width, out.shape[3], out.shape[4]
+    frames = pixels // area
     shard = where_ref[2]
-
-    place = lax.broadcasted_iota(jnp.int32, (1, pixels), 1)
-    row, col = (place % area) // width, place % width
-    masks = {}
-    for a in range(SIDE):
-        for b in range(SIDE):
-            r, c = row + a - 1, col + b - 1
-            masks[a, b] = ((r >= 0) & (r < rows) & (c >= 0) & (c < width)).astype(jnp.float32)
+    lens = [where_ref[PLACES + i] for i in range(clips)]
+    col = lax.broadcasted_iota(jnp.int32, (1, pixels), 1) % width
+    left, right = (col > 0).astype(jnp.float32), (col < width - 1).astype(jnp.float32)
 
     lane = pl.ds(pl.multiple_of((shard % 2) * chans, chans), chans)
     for offset in range(blocks):
         block = shard ^ offset
         value = turned_refs[offset][lane, :].astype(jnp.float32)
-        for a in range(SIDE):
-            for b in range(SIDE):
-                step = (a - 1) * width + b - 1
-                copy = value if step == 0 else pltpu.roll(value, (-step) % pixels, 1) * masks[a, b]
-                copy = copy.astype(taps.dtype)
-                at = (SIDE * a + b) * chans
+        copies = (pltpu.roll(value, 1, 1) * left, value, pltpu.roll(value, pixels - 1, 1) * right)
+        for b, copy in enumerate(copies):
+            copy = copy.astype(taps.dtype)
+            for f in range(frames):
+                taps[block * frames + f, b * chans : (b + 1) * chans] = copy[:, f * area : (f + 1) * area]
+    edge = jnp.zeros((width, outs), cots[0].dtype)
+    for start in range(0, blocks, group):
+        offsets = range(start, start + group)
+        pieces = []
+        for offset in offsets:
+            for f in range(frames):
+                frame = (shard ^ offset) * frames + f
+                first = first_of(lens, clips, frame)
+                sources = [jnp.maximum(frame - lag, first) for lag in range(LAGS)]
+                pieces.append(jnp.concatenate([taps[source] for source in sources], axis=0))
+        pieces = jnp.concatenate(pieces, axis=1)
+        for row_step in range(SIDE):
+            values = []
+            for offset in offsets:
                 for f in range(frames):
-                    taps[block * frames + f, at : at + chans] = copy[:, f * area : (f + 1) * area]
-    for offset in range(blocks):
-        first = (shard ^ offset) * frames
-
-        def lagged(lag, carry, offset=offset, first=first):
-            pieces = []
-            for f in range(frames):
-                frame = first + f
-                source = jnp.maximum(frame - lag, first_of(lens, clips, frame))
-                pieces.append(taps[source])
-            terms = jnp.dot(jnp.concatenate(pieces, axis=1), cots[offset][...], preferred_element_type=jnp.float32)
-            at = pl.ds(lag * SIDE * SIDE, SIDE * SIDE)
-            terms = terms.reshape(SIDE * SIDE, chans, terms.shape[1])
-            if offset == 0:
-                out[at] = terms
-            elif offset == blocks - 1:
-                out[at] = (out[at] + terms) * scale
-            else:
-                out[at] += terms
-            return carry
-
-        lax.fori_loop(0, LAGS, lagged, 0)
-
-
-def weight_terms(where, lens, turned_blocks, cots, rows, width, scale):
+                    top, end = f * area, (f + 1) * area
+                    if row_step == 0:
+                        values += [cots[offset][top + width : end], edge]
+                    elif row_step == 1:
+                        values += [cots[offset][top:end]]
+                    else:
+                        values += [edge, cots[offset][top : end - width]]
+            terms = jnp.dot(pieces, jnp.concatenate(values, axis=0), preferred_element_type=jnp.float32)
+            terms = terms.reshape(LAGS, SIDE, chans, outs)
+            if start:
+                terms = terms + out[:, row_step]
+            out[:, row_step] = terms * scale if start + group == blocks else terms
+
+
+def weight_terms(where, turned_blocks, cots, rows, width, scale, group=2):
     blocks, pixels = len(cots), cots[0].shape[0]
     chans = turned_blocks[0].shape[0] // 2
-    area = rows * width
-    frames = pixels // area
     outs = cots[0].shape[1]
     whole = pl.BlockSpec(memory_space=pltpu.VMEM)
     smem = pl.BlockSpec(memory_space=pltpu.SMEM)
-    taps = SIDE * SIDE
-    return pl.pallas_call(
-        functools.partial(weight_body, blocks, frames, rows, width, lens.shape[0], scale),
-        out_shape=jax.ShapeDtypeStruct((LAGS * taps, chans, outs), jnp.float32),
-        in_specs=[smem, smem] + [whole] * (2 * blocks),
+    taps = LAGS * SIDE * SIDE
+    frames = pixels // (rows * width)
+    result = pl.pallas_call(
+        functools.partial(weight_body, blocks, group, rows, width, where.shape[0] - PLACES, scale),
+        out_shape=jax.ShapeDtypeStruct((LAGS, SIDE, SIDE, chans, outs), jnp.float32),
+        in_specs=[smem] + [whole] * (2 * blocks),
         out_specs=whole,
-        scratch_shapes=[pltpu.VMEM((blocks * frames, taps * chans, area), turned_blocks[0].dtype)],
-        compiler_params=pltpu.CompilerParams(vmem_limit_bytes=28 << 20),
+        scratch_shapes=[pltpu.VMEM((blocks * frames, SIDE * chans, rows * width), turned_blocks[0].dtype)],
+        compiler_params=pltpu.CompilerParams(vmem_limit_bytes=8 << 20),
         cost_estimate=pl.CostEstimate(
-            flops=2 * blocks * pixels * LAGS * taps * chans * outs, transcendentals=0, bytes_accessed=8 << 20),
+            flops=2 * blocks * pixels * taps * chans * outs, transcendentals=0, bytes_accessed=8 << 20),
         name="weight_terms",
-    )(where, lens, *turned_blocks, *cots)
+    )(where, *turned_blocks, *cots)
+    return result.reshape(taps, chans, outs)
 
 
 def extended_2(cells, sides, width):
@@ -475,7 +493,7 @@
     pixels = frames * rows * width
     weights = pltpu.with_memory_space_constraint(weights, pltpu.HBM)
     shard, chan = lax.axis_index("tm"), lax.axis_index("chan")
-    where = jnp.stack([shard * frames, chan, shard]).astype(jnp.int32)
+    where = jnp.concatenate([jnp.stack([shard * frames, chan, shard]), lengths]).astype(jnp.int32)
     scaled = video.astype(jnp.float32) * channel_gain
     activated = silu(video.reshape(pixels, chans), channel_gain).reshape(video.shape)
     own = [activated] + [ahead(activated, "chan", j) for j in range(1, parts)]
@@ -483,7 +501,7 @@
     past = [before] + [ahead(before, "chan", j) for j in range(1, parts)]
     later = along(cotangent, "tm", -1)
     cots = gathered_blocks(cotangent.reshape(pixels, chans), "tm")
-    mine, *others = backward(where, lengths, cotangent, later, weights)
+    mine, *others = backward(where, cotangent, later, weights)
     act_grad = mine
     for j in range(1, parts):
         act_grad = act_grad + ahead(others[j - 1], "chan", parts - j).astype(jnp.float32)
@@ -492,12 +510,12 @@
     for offset in range(shards // 2):
         block = across(sent[offset], "tm", 2 * offset) if offset else sent[0]
         blocks += [block, across(block, "tm", 1)]
-    output = forward(where, lengths, video, own, past, weights)
+    output = forward(where, video, own, past, weights)
     sigmoid_value = jax.nn.sigmoid(scaled)
     slope_factor = sigmoid_value * (1.0 + scaled * (1.0 - sigmoid_value))
     input_grad = (cotangent.astype(jnp.float32) + act_grad * slope_factor * channel_gain).astype(jnp.bfloat16)
     scale = 1.0 / math.sqrt(pixels * shards)
-    weight_grad = weight_terms(where, lengths, blocks, cots, rows, width, scale)
+    weight_grad = weight_terms(where, blocks, cots, rows, width, scale)
     return (output, input_grad, weight_grad)
 
 

time: 66 us -> 54.9 us (0.83)
  Pallas kernels: 34 us -> 21.2 us
  waiting for transfers between devices: 3.85 us -> 8.41 us
  starting transfers between devices: 22.3 us -> 19.9 us
    pallas_call x3, Pallas kernels: 30.1 us -> 20.3 us  [the longest x1 7.41 us: forward(): pl.pallas_call(functools.partial(forward_body, parts, where.shape[0] - PL...]
    ppermute x14, waiting for transfers between devices: 3.84 us -> 8.39 us  [across(): lax.ppermute(value, axis, [(i, i ^ offset) for i in range(lax.axis_size(a...]
    ppermute x14, starting transfers between devices: 14.5 us -> 12.1 us  [across(): lax.ppermute(value, axis, [(i, i ^ offset) for i in range(lax.axis_size(a...]
    pallas_call x1, Pallas kernels: 1.81 us -> 0.16 us  [silu(): pl.pallas_call(silu_body, out_shape=jax.ShapeDtypeStruct(video.shape, vid...]
    pallas_call x1, Pallas kernels: 2.02 us -> 0.76 us  [turned(): pl.pallas_call(functools.partial(turned_body, len(own)), out_shape=[jax.S...]
    concatenate x0 -> x1, other arithmetic: none -> 0.73 us  [whole_rows(): jnp.concatenate([jnp.stack([shard * frames, chan, shard]), lengths])]
    unnamed x26 -> x10, local copies, waits for them, and re-layouts: 3 us -> 2.59 us
  transfers between devices with their start and end apart: 19 -> 19, of which waited for: 2 -> 4; matrix products, arithmetic and copies ran while one was open for 3% -> 3% of each run, Pallas kernels for 33% -> 28%
where the time goes in v1:
time: 54.9 us; the launch traced here: 54.7 us
  Pallas kernels  21.2 us (39%)
  starting transfers between devices  19.9 us (36%)
  waiting for transfers between devices  8.41 us (15%)
  local copies, waits for them, and re-layouts  2.59 us (5%)
  other arithmetic  1.74 us (3%)
  between operations  0.75 us (1%)
    ppermute x14, starting transfers between devices, across(): lax.ppermute(value, axis, [(i, i ^ offset) for i in range(lax.axis_size(a...  12.1 us
    ppermute x14, waiting for transfers between devices, across(): lax.ppermute(value, axis, [(i, i ^ offset) for i in range(lax.axis_size(a...  8.39 us
    pallas_call x1, Pallas kernels, forward(): pl.pallas_call(functools.partial(forward_body, parts, where.shape[0] - PL...  7.41 us
    pallas_call x1, Pallas kernels, backward(): pl.pallas_call(functools.partial(backward_body, parts, where.shape[0] - P...  6.89 us
    pallas_call x1, Pallas kernels, weight_terms(): pl.pallas_call(functools.partial(weight_body, blocks, group, rows, width,...  6 us
    ppermute x3, starting transfers between devices, ahead(): lax.ppermute(value, axis, [((i + steps) % count, i) for i in range(count)])  5.06 us
    ppermute x2, starting transfers between devices, along(): lax.ppermute(value, axis, [(source, source + steps) for source in range(f...  2.74 us
    unnamed x10, local copies, waits for them, and re-layouts  2.59 us
  transfers between devices with their start and end apart: 19, of which 4 were waited for; matrix products, arithmetic and copies ran while one was open for 3% of the time, Pallas kernels for 28%

profile of v1, /device:TPU:0, one launch (start us, length us, event | category | flops | bytes accessed | tf_op | source)
XLA Modules:
  0.0 54.7 jit_solution(7322035561861284228)
XLA Ops:
  0.6 0.0 copy-start
  0.6 0.9 %copy-done = bf16[2,8,32,256]{3,2,1,0:T(8,128)(2,1)S(1)} copy-done((bf16[2,8,32,256]{3,2,1,0:T(8,128)(2,1)S(1)}, bf16[2,8,32,256]{3,2,1,0:T(8,128)(2,1)}, u32[]{:S(2)}) %copy-start) | copy-done | bytes 262168
  1.6 0.7 %copy-done.3 = f32[256]{0:T(256)S(1)} copy-done((f32[256]{0:T(256)S(1)}, f32[256]{0:T(256)}, u32[]{:S(2)}) %copy-start.3) | copy-done | bytes 1048
  2.3 0.2 silu.1.refs_0_
  2.4 0.0 copy-start.1
  2.4 3.0 %collective-permute-start = (bf16[2,8,32,256]{3,2,1,0:T(8,128)(2,1)S(1)}, bf16[2,8,32,256]{3,2,1,0:T(8,128)(2,1)S(1)}, u32[]{:S(2)}, u32[]{:S(2)}) collective-permute-start(bf16[2,8,32,256]{3,2,1,0:T(8,128)(2,1)S(1)} %bitcast.9), channel_id=1, source_target_pairs={{1,0},{0,1},{3,2},{2,3},{5,4},{4,5},{7,6},{6,7},{9,8},{8,9},{11,10... | collective-permute-start | bytes 786440 | tf_op jit(solution)/shard_map/ppermute | solution.py:476
  5.5 1.5 %collective-permute-start.1 = (bf16[2,8,32,256]{3,2,1,0:T(8,128)(2,1)S(1)}, bf16[2,8,32,256]{3,2,1,0:T(8,128)(2,1)S(1)}, u32[]{:S(2)}, u32[]{:S(2)}) collective-permute-start(bf16[2,8,32,256]{3,2,1,0:T(8,128)(2,1)S(1)} %bitcast.10), channel_id=1, source_target_pairs={{0,2},{2,4},{4,6},{6,8},{8,10},{10,12},{12,14},{1,3},{3,5},{5,7},{... | collective-permute-start | bytes 786440 | tf_op jit(solution)/shard_map/ppermute | solution.py:467
  6.9 3.1 %collective-permute-start.15 = (bf16[512,256]{1,0:T(8,128)(2,1)}, bf16[512,256]{1,0:T(8,128)(2,1)S(1)}, u32[]{:S(2)}, u32[]{:S(2)}) collective-permute-start(bf16[512,256]{1,0:T(8,128)(2,1)} %bitcast.14), channel_id=1, source_target_pairs={{0,8},{2,10},{4,12},{6,14},{8,0},{10,2},{12,4},{14,6},{1,9},{3,11}... | collective-permute-start | bytes 786440 | tf_op jit(solution)/shard_map/ppermute | solution.py:471
  10.0 1.3 %collective-permute-start.3 = (bf16[2,8,32,256]{3,2,1,0:T(8,128)(2,1)}, bf16[2,8,32,256]{3,2,1,0:T(8,128)(2,1)S(1)}, u32[]{:S(2)}, u32[]{:S(2)}) collective-permute-start(bf16[2,8,32,256]{3,2,1,0:T(8,128)(2,1)} %own.1), channel_id=1, source_target_pairs={{2,0},{4,2},{6,4},{8,6},{10,8},{12,10},{14,12},{3,1},{5,3},{7,5},{... | collective-permute-start | bytes 786440 | tf_op jit(solution)/shard_map/ppermute | solution.py:467
  11.3 3.7 %collective-permute-start.13 = (bf16[512,256]{1,0:T(8,128)(2,1)}, bf16[512,256]{1,0:T(8,128)(2,1)S(1)}, u32[]{:S(2)}, u32[]{:S(2)}) collective-permute-start(bf16[512,256]{1,0:T(8,128)(2,1)} %bitcast.15), channel_id=1, source_target_pairs={{0,4},{2,6},{4,0},{6,2},{8,12},{10,14},{12,8},{14,10},{1,5},{3,7},... | collective-permute-start | bytes 786440 | tf_op jit(solution)/shard_map/ppermute | solution.py:471
  15.0 0.7 %pad_add_fusion.where_ref = s32[7]{0:T(128)S(1)} fusion(s32[4]{0:T(128)} %param.8, s32[1]{0:T(128)} %bitcast.2, s32[1]{0:T(128)} %bitcast.1, s32[1]{0:T(128)} %bitcast), kind=kLoop, calls=%fused_computation.1 | loop fusion | flops 21 | bytes 56 | tf_op jit(solution)/shard_map/concatenate | solution.py:496
  15.8 0.0 collective-permute-done.refs_1_
  15.8 0.0 collective-permute-start.12
  15.8 0.8 %turned.1 = (bf16[128,512]{1,0:T(8,128)(2,1)S(1)}, bf16[128,512]{1,0:T(8,128)(2,1)S(1)}, bf16[128,512]{1,0:T(8,128)(2,1)S(1)}, bf16[128,512]{1,0:T(8,128)(2,1)S(1)}) custom-call(s32[7]{0:T(128)S(1)} %pad_add_fusion.where_ref, bf16[512,256]{1,0:T(8,128)(2,1)S(1)} %silu.1.refs_0_, bf16[512,256]{1,0:T(8,128)(2,1)S(1)} %bitcast.13), custom_call_target="tpu_custom_call" | custom-call | flops 8388608 | bytes 524288 | tf_op jit(solution)/shard_map/turned/pallas_call | solution.py:221
  16.6 0.0 collective-permute-done.1.refs_2_
  16.6 0.2 collective-permute-start.6
  16.7 5.3 %collective-permute-done.15.refs_12_ = bf16[512,256]{1,0:T(8,128)(2,1)S(1)} collective-permute-done((bf16[512,256]{1,0:T(8,128)(2,1)}, bf16[512,256]{1,0:T(8,128)(2,1)S(1)}, u32[]{:S(2)}, u32[]{:S(2)}) %collective-permute-start.15) | collective-permute-done | bytes 262176 | tf_op jit(solution)/shard_map/ppermute | solution.py:471
  22.1 0.2 collective-permute-start.8
  22.3 0.0 collective-permute-done.3.later
  22.3 0.5 collective-permute-start.2
  22.9 0.9 %copy-done.2 = bf16[2,8,32,256]{3,2,1,0:T(8,128)(2,1)S(1)} copy-done((bf16[2,8,32,256]{3,2,1,0:T(8,128)(2,1)S(1)}, bf16[2,8,32,256]{3,2,1,0:T(8,128)(2,1)}, u32[]{:S(2)}) %copy-start.2) | copy-done | bytes 262168
  23.8 6.9 %backward.1 = (f32[2,8,32,256]{3,2,1,0:T(8,128)S(1)}, bf16[2,8,32,256]{3,2,1,0:T(8,128)(2,1)S(1)}) custom-call(s32[7]{0:T(128)S(1)} %pad_add_fusion.where_ref, bf16[2,8,32,256]{3,2,1,0:T(8,128)(2,1)S(1)} %copy-done.2, bf16[2,8,32,256]{3,2,1,0:T(8,128)(2,1)S(1)} %collective-permute-done.3.later, bf16[27,512,256]{2,1,0:T(8,128)(2,1)} %weights.1), custom_call_target="tpu_custom_call" | custom-call | flops 3623878656 | bytes 7077888 | tf_op jit(solution)/shard_map/backward/pallas_call | solution.py:186
  30.7 0.0 copy-start.4
  30.7 2.3 %collective-permute-done.13.refs_10_ = bf16[512,256]{1,0:T(8,128)(2,1)S(1)} collective-permute-done((bf16[512,256]{1,0:T(8,128)(2,1)}, bf16[512,256]{1,0:T(8,128)(2,1)S(1)}, u32[]{:S(2)}, u32[]{:S(2)}) %collective-permute-start.13) | collective-permute-done | bytes 262176 | tf_op jit(solution)/shard_map/ppermute | solution.py:471
  33.0 2.4 %collective-permute-start.10 = (bf16[128,512]{1,0:T(8,128)(2,1)S(1)}, bf16[128,512]{1,0:T(8,128)(2,1)S(1)}, u32[]{:S(2)}, u32[]{:S(2)}) collective-permute-start(bf16[128,512]{1,0:T(8,128)(2,1)S(1)} %get-tuple-element.14), channel_id=1, source_target_pairs={{0,12},{2,14},{4,8},{6,10},{8,4},{10,6},{12,0},{14,2},{1,13},{3,15... | collective-permute-start | bytes 393224 | tf_op jit(solution)/shard_map/ppermute | solution.py:471
  35.5 0.0 collective-permute-done.12.refs_9_
  35.5 0.2 collective-permute-start.5
  35.7 0.0 collective-permute-done.6.refs_2_
  35.7 1.5 %collective-permute-start.4 = (bf16[2,8,32,256]{3,2,1,0:T(8,128)(2,1)S(1)}, bf16[2,8,32,256]{3,2,1,0:T(8,128)(2,1)S(1)}, u32[]{:S(2)}, u32[]{:S(2)}) collective-permute-start(bf16[2,8,32,256]{3,2,1,0:T(8,128)(2,1)S(1)} %get-tuple-element.10), channel_id=1, source_target_pairs={{1,0},{0,1},{3,2},{2,3},{5,4},{4,5},{7,6},{6,7},{9,8},{8,9},{11,10... | collective-permute-start | bytes 786440 | tf_op jit(solution)/shard_map/ppermute | solution.py:476
  37.2 0.0 collective-permute-done.8.refs_4_
  37.2 0.6 %collective-permute-start.17 = (bf16[512,256]{1,0:T(8,128)(2,1)S(1)}, bf16[512,256]{1,0:T(8,128)(2,1)S(1)}, u32[]{:S(2)}, u32[]{:S(2)}) collective-permute-start(bf16[512,256]{1,0:T(8,128)(2,1)S(1)} %collective-permute-done.15.refs_12_), channel_id=1, source_target_pairs={{0,4},{2,6},{4,0},{6,2},{8,12},{10,14},{12,8},{14,10},{1,5},{3,7},... | collective-permute-start | bytes 786440 | tf_op jit(solution)/shard_map/ppermute | solution.py:471
  37.9 0.0 collective-permute-done.2.refs_3_
  37.9 0.0 collective-permute-start.7
  37.9 7.4 %forward.1 = bf16[2,8,32,256]{3,2,1,0:T(8,128)(2,1)} custom-call(s32[7]{0:T(128)S(1)} %pad_add_fusion.where_ref, bf16[2,8,32,256]{3,2,1,0:T(8,128)(2,1)S(1)} %copy-done.1, bf16[2,8,32,256]{3,2,1,0:T(8,128)(2,1)S(1)} %bitcast.11, bf16[2,8,32,256]{3,2,1,0:T(8,128)(2,1)S(1)} %collective-permute-done.refs_1_, ...), custom_call_target="tpu_custom_call" | custom-call | flops 3623878656 | bytes 7077888 | tf_op jit(solution)/shard_map/forward/pallas_call | solution.py:122
  45.3 0.0 collective-permute-done.10.refs_6_
  45.3 0.6 %collective-permute-start.16 = (bf16[512,256]{1,0:T(8,128)(2,1)S(1)}, bf16[512,256]{1,0:T(8,128)(2,1)S(1)}, u32[]{:S(2)}, u32[]{:S(2)}) collective-permute-start(bf16[512,256]{1,0:T(8,128)(2,1)S(1)} %collective-permute-done.15.refs_12_), channel_id=1, source_target_pairs={{0,2},{2,0},{4,6},{6,4},{8,10},{10,8},{12,14},{14,12},{1,3},{3,1},... | collective-permute-start | bytes 786440 | tf_op jit(solution)/shard_map/ppermute | solution.py:471
  45.9 0.0 collective-permute-done.5.refs_1_
  45.9 0.1 collective-permute-start.14
  46.0 0.0 collective-permute-done.7.refs_3_
  46.0 0.4 collective-permute-start.9
  46.4 0.5 collective-permute-done.17.refs_14_
  46.9 0.0 collective-permute-start.11
  47.0 0.0 collective-permute-done.4
  47.0 0.5 collective-permute-start.18
  47.4 1.0 %add_convert_fusion = bf16[2,8,32,256]{3,2,1,0:T(8,128)(2,1)} fusion(bf16[2,8,32,256]{3,2,1,0:T(8,128)(2,1)S(1)} %copy-done.1, f32[2,8,32,256]{3,2,1,0:T(8,128)S(1)} %get-tuple-element.9, bf16[2,8,32,256]{3,2,1,0:T(8,128)(2,1)S(1)} %collective-permute-done.4, bf16[2,8,32,256]{3,2,1,0:T(8,128)(2,1)S(1)} %copy-done.2, f32[256]{0:T(256)S(1)} %copy-done.4), kind=kLoop, calls=%fused_computation | loop fusion | flops 2097152 | bytes 1573888 | tf_op jit(solution)/shard_map/convert_element_type | solution.py:516
  48.5 0.0 collective-permute-done.14.refs_11_
  48.5 0.2 collective-permute-done.18.refs_15_
  48.7 6.0 %weight_terms.1 = f32[3,3,3,64,256]{4,3,2,1,0:T(8,128)} custom-call(s32[7]{0:T(128)S(1)} %pad_add_fusion.where_ref, bf16[128,512]{1,0:T(8,128)(2,1)S(1)} %get-tuple-element.11.refs_0_, bf16[128,512]{1,0:T(8,128)(2,1)S(1)} %collective-permute-done.5.refs_1_, bf16[128,512]{1,0:T(8,128)(2,1)S(1)} %collective-permute-done.6.refs_2_, ...), custom_call_target="tpu_custom_call" | custom-call | flops 3623878656 | bytes 8388608 | tf_op jit(solution)/shard_map/weight_terms/pallas_call | solution.py:289
  (7 shorter events, 0.0 us)
Async XLA Ops:
  0.6 1.0 %copy-start = (bf16[2,8,32,256]{3,2,1,0:T(8,128)(2,1)S(1)}, bf16[2,8,32,256]{3,2,1,0:T(8,128)(2,1)}, u32[]{:S(2)}) copy-start(bf16[2,8,32,256]{3,2,1,0:T(8,128)(2,1)} %video.1) | copy-start | bytes 786436
  1.6 0.7 %copy-start.3 = (f32[256]{0:T(256)S(1)}, f32[256]{0:T(256)}, u32[]{:S(2)}) copy-start(f32[256]{0:T(256)} %param.6) | copy-start | bytes 3076
  2.4 35.4 %copy-start.1 = (bf16[2,8,32,256]{3,2,1,0:T(8,128)(2,1)S(1)}, bf16[2,8,32,256]{3,2,1,0:T(8,128)(2,1)}, u32[]{:S(2)}) copy-start(bf16[2,8,32,256]{3,2,1,0:T(8,128)(2,1)} %video.1) | copy-start | bytes 786436
  2.4 13.3 %collective-permute-start = (bf16[2,8,32,256]{3,2,1,0:T(8,128)(2,1)S(1)}, bf16[2,8,32,256]{3,2,1,0:T(8,128)(2,1)S(1)}, u32[]{:S(2)}, u32[]{:S(2)}) collective-permute-start(bf16[2,8,32,256]{3,2,1,0:T(8,128)(2,1)S(1)} %bitcast.9), channel_id=1, source_target_pairs={{1,0},{0,1},{3,2},{2,3},{5,4},{4,5},{7,6},{6,7},{9,8},{8,9},{11,10... | collective-permute-start | bytes 786440 | tf_op jit(solution)/shard_map/ppermute | solution.py:476
  5.5 11.1 %collective-permute-start.1 = (bf16[2,8,32,256]{3,2,1,0:T(8,128)(2,1)S(1)}, bf16[2,8,32,256]{3,2,1,0:T(8,128)(2,1)S(1)}, u32[]{:S(2)}, u32[]{:S(2)}) collective-permute-start(bf16[2,8,32,256]{3,2,1,0:T(8,128)(2,1)S(1)} %bitcast.10), channel_id=1, source_target_pairs={{0,2},{2,4},{4,6},{6,8},{8,10},{10,12},{12,14},{1,3},{3,5},{5,7},{... | collective-permute-start | bytes 786440 | tf_op jit(solution)/shard_map/ppermute | solution.py:467
  6.9 15.2 %collective-permute-start.15 = (bf16[512,256]{1,0:T(8,128)(2,1)}, bf16[512,256]{1,0:T(8,128)(2,1)S(1)}, u32[]{:S(2)}, u32[]{:S(2)}) collective-permute-start(bf16[512,256]{1,0:T(8,128)(2,1)} %bitcast.14), channel_id=1, source_target_pairs={{0,8},{2,10},{4,12},{6,14},{8,0},{10,2},{12,4},{14,6},{1,9},{3,11}... | collective-permute-start | bytes 786440 | tf_op jit(solution)/shard_map/ppermute | solution.py:471
  10.0 12.3 %collective-permute-start.3 = (bf16[2,8,32,256]{3,2,1,0:T(8,128)(2,1)}, bf16[2,8,32,256]{3,2,1,0:T(8,128)(2,1)S(1)}, u32[]{:S(2)}, u32[]{:S(2)}) collective-permute-start(bf16[2,8,32,256]{3,2,1,0:T(8,128)(2,1)} %own.1), channel_id=1, source_target_pairs={{2,0},{4,2},{6,4},{8,6},{10,8},{12,10},{14,12},{3,1},{5,3},{7,5},{... | collective-permute-start | bytes 786440 | tf_op jit(solution)/shard_map/ppermute | solution.py:467
  11.3 21.7 %collective-permute-start.13 = (bf16[512,256]{1,0:T(8,128)(2,1)}, bf16[512,256]{1,0:T(8,128)(2,1)S(1)}, u32[]{:S(2)}, u32[]{:S(2)}) collective-permute-start(bf16[512,256]{1,0:T(8,128)(2,1)} %bitcast.15), channel_id=1, source_target_pairs={{0,4},{2,6},{4,0},{6,2},{8,12},{10,14},{12,8},{14,10},{1,5},{3,7},... | collective-permute-start | bytes 786440 | tf_op jit(solution)/shard_map/ppermute | solution.py:471
  15.8 19.7 %collective-permute-start.12 = (bf16[512,256]{1,0:T(8,128)(2,1)}, bf16[512,256]{1,0:T(8,128)(2,1)S(1)}, u32[]{:S(2)}, u32[]{:S(2)}) collective-permute-start(bf16[512,256]{1,0:T(8,128)(2,1)} %bitcast.16), channel_id=1, source_target_pairs={{0,2},{2,0},{4,6},{6,4},{8,10},{10,8},{12,14},{14,12},{1,3},{3,1},... | collective-permute-start | bytes 786440 | tf_op jit(solution)/shard_map/ppermute | solution.py:471
  16.6 19.1 %collective-permute-start.6 = (bf16[128,512]{1,0:T(8,128)(2,1)S(1)}, bf16[128,512]{1,0:T(8,128)(2,1)S(1)}, u32[]{:S(2)}, u32[]{:S(2)}) collective-permute-start(bf16[128,512]{1,0:T(8,128)(2,1)S(1)} %get-tuple-element.12), channel_id=1, source_target_pairs={{0,4},{2,6},{4,0},{6,2},{8,12},{10,14},{12,8},{14,10},{1,5},{3,7},... | collective-permute-start | bytes 393224 | tf_op jit(solution)/shard_map/ppermute | solution.py:471
  22.1 15.1 %collective-permute-start.8 = (bf16[128,512]{1,0:T(8,128)(2,1)S(1)}, bf16[128,512]{1,0:T(8,128)(2,1)S(1)}, u32[]{:S(2)}, u32[]{:S(2)}) collective-permute-start(bf16[128,512]{1,0:T(8,128)(2,1)S(1)} %get-tuple-element.13), channel_id=1, source_target_pairs={{0,8},{2,10},{4,12},{6,14},{8,0},{10,2},{12,4},{14,6},{1,9},{3,11}... | collective-permute-start | bytes 393224 | tf_op jit(solution)/shard_map/ppermute | solution.py:471
  22.3 15.5 %collective-permute-start.2 = (bf16[2,8,32,256]{3,2,1,0:T(8,128)(2,1)S(1)}, bf16[2,8,32,256]{3,2,1,0:T(8,128)(2,1)S(1)}, u32[]{:S(2)}, u32[]{:S(2)}) collective-permute-start(bf16[2,8,32,256]{3,2,1,0:T(8,128)(2,1)S(1)} %collective-permute-done.1.refs_2_), channel_id=1, source_target_pairs={{1,0},{0,1},{3,2},{2,3},{5,4},{4,5},{7,6},{6,7},{9,8},{8,9},{11,10... | collective-permute-start | bytes 786440 | tf_op jit(solution)/shard_map/ppermute | solution.py:476
  22.9 0.9 %copy-start.2 = (bf16[2,8,32,256]{3,2,1,0:T(8,128)(2,1)S(1)}, bf16[2,8,32,256]{3,2,1,0:T(8,128)(2,1)}, u32[]{:S(2)}) copy-start(bf16[2,8,32,256]{3,2,1,0:T(8,128)(2,1)} %own.1) | copy-start | bytes 786436
  30.7 16.7 %copy-start.4 = (f32[256]{0:T(256)S(1)}, f32[256]{0:T(256)}, u32[]{:S(2)}) copy-start(f32[256]{0:T(256)} %param.6) | copy-start | bytes 3076
  33.0 12.3 %collective-permute-start.10 = (bf16[128,512]{1,0:T(8,128)(2,1)S(1)}, bf16[128,512]{1,0:T(8,128)(2,1)S(1)}, u32[]{:S(2)}, u32[]{:S(2)}) collective-permute-start(bf16[128,512]{1,0:T(8,128)(2,1)S(1)} %get-tuple-element.14), channel_id=1, source_target_pairs={{0,12},{2,14},{4,8},{6,10},{8,4},{10,6},{12,0},{14,2},{1,13},{3,15... | collective-permute-start | bytes 393224 | tf_op jit(solution)/shard_map/ppermute | solution.py:471
  35.5 10.4 %collective-permute-start.5 = (bf16[128,512]{1,0:T(8,128)(2,1)S(1)}, bf16[128,512]{1,0:T(8,128)(2,1)S(1)}, u32[]{:S(2)}, u32[]{:S(2)}) collective-permute-start(bf16[128,512]{1,0:T(8,128)(2,1)S(1)} %get-tuple-element.11.refs_0_), channel_id=1, source_target_pairs={{0,2},{2,0},{4,6},{6,4},{8,10},{10,8},{12,14},{14,12},{1,3},{3,1},... | collective-permute-start | bytes 393224 | tf_op jit(solution)/shard_map/ppermute | solution.py:471
  35.7 11.2 %collective-permute-start.4 = (bf16[2,8,32,256]{3,2,1,0:T(8,128)(2,1)S(1)}, bf16[2,8,32,256]{3,2,1,0:T(8,128)(2,1)S(1)}, u32[]{:S(2)}, u32[]{:S(2)}) collective-permute-start(bf16[2,8,32,256]{3,2,1,0:T(8,128)(2,1)S(1)} %get-tuple-element.10), channel_id=1, source_target_pairs={{1,0},{0,1},{3,2},{2,3},{5,4},{4,5},{7,6},{6,7},{9,8},{8,9},{11,10... | collective-permute-start | bytes 786440 | tf_op jit(solution)/shard_map/ppermute | solution.py:476
  37.2 9.7 %collective-permute-start.17 = (bf16[512,256]{1,0:T(8,128)(2,1)S(1)}, bf16[512,256]{1,0:T(8,128)(2,1)S(1)}, u32[]{:S(2)}, u32[]{:S(2)}) collective-permute-start(bf16[512,256]{1,0:T(8,128)(2,1)S(1)} %collective-permute-done.15.refs_12_), channel_id=1, source_target_pairs={{0,4},{2,6},{4,0},{6,2},{8,12},{10,14},{12,8},{14,10},{1,5},{3,7},... | collective-permute-start | bytes 786440 | tf_op jit(solution)/shard_map/ppermute | solution.py:471
  37.9 8.1 %collective-permute-start.7 = (bf16[128,512]{1,0:T(8,128)(2,1)S(1)}, bf16[128,512]{1,0:T(8,128)(2,1)S(1)}, u32[]{:S(2)}, u32[]{:S(2)}) collective-permute-start(bf16[128,512]{1,0:T(8,128)(2,1)S(1)} %collective-permute-done.6.refs_2_), channel_id=1, source_target_pairs={{0,2},{2,0},{4,6},{6,4},{8,10},{10,8},{12,14},{14,12},{1,3},{3,1},... | collective-permute-start | bytes 393224 | tf_op jit(solution)/shard_map/ppermute | solution.py:471
  45.3 3.2 %collective-permute-start.16 = (bf16[512,256]{1,0:T(8,128)(2,1)S(1)}, bf16[512,256]{1,0:T(8,128)(2,1)S(1)}, u32[]{:S(2)}, u32[]{:S(2)}) collective-permute-start(bf16[512,256]{1,0:T(8,128)(2,1)S(1)} %collective-permute-done.15.refs_12_), channel_id=1, source_target_pairs={{0,2},{2,0},{4,6},{6,4},{8,10},{10,8},{12,14},{14,12},{1,3},{3,1},... | collective-permute-start | bytes 786440 | tf_op jit(solution)/shard_map/ppermute | solution.py:471
  45.9 2.6 %collective-permute-start.14 = (bf16[512,256]{1,0:T(8,128)(2,1)S(1)}, bf16[512,256]{1,0:T(8,128)(2,1)S(1)}, u32[]{:S(2)}, u32[]{:S(2)}) collective-permute-start(bf16[512,256]{1,0:T(8,128)(2,1)S(1)} %collective-permute-done.13.refs_10_), channel_id=1, source_target_pairs={{0,2},{2,0},{4,6},{6,4},{8,10},{10,8},{12,14},{14,12},{1,3},{3,1},... | collective-permute-start | bytes 786440 | tf_op jit(solution)/shard_map/ppermute | solution.py:471
  46.0 2.5 %collective-permute-start.9 = (bf16[128,512]{1,0:T(8,128)(2,1)S(1)}, bf16[128,512]{1,0:T(8,128)(2,1)S(1)}, u32[]{:S(2)}, u32[]{:S(2)}) collective-permute-start(bf16[128,512]{1,0:T(8,128)(2,1)S(1)} %collective-permute-done.8.refs_4_), channel_id=1, source_target_pairs={{0,2},{2,0},{4,6},{6,4},{8,10},{10,8},{12,14},{14,12},{1,3},{3,1},... | collective-permute-start | bytes 393224 | tf_op jit(solution)/shard_map/ppermute | solution.py:471
  46.9 1.5 %collective-permute-start.11 = (bf16[128,512]{1,0:T(8,128)(2,1)S(1)}, bf16[128,512]{1,0:T(8,128)(2,1)S(1)}, u32[]{:S(2)}, u32[]{:S(2)}) collective-permute-start(bf16[128,512]{1,0:T(8,128)(2,1)S(1)} %collective-permute-done.10.refs_6_), channel_id=1, source_target_pairs={{0,2},{2,0},{4,6},{6,4},{8,10},{10,8},{12,14},{14,12},{1,3},{3,1},... | collective-permute-start | bytes 393224 | tf_op jit(solution)/shard_map/ppermute | solution.py:471
  47.0 1.7 %collective-permute-start.18 = (bf16[512,256]{1,0:T(8,128)(2,1)S(1)}, bf16[512,256]{1,0:T(8,128)(2,1)S(1)}, u32[]{:S(2)}, u32[]{:S(2)}) collective-permute-start(bf16[512,256]{1,0:T(8,128)(2,1)S(1)} %collective-permute-done.17.refs_14_), channel_id=1, source_target_pairs={{0,2},{2,0},{4,6},{6,4},{8,10},{10,8},{12,14},{14,12},{1,3},{3,1},... | collective-permute-start | bytes 786440 | tf_op jit(solution)/shard_map/ppermute | solution.py:471

commit v2 on v1

--- a/solution.py
+++ b/solution.py
@@ -61,28 +61,12 @@
     )(video, gain.reshape(1, -1))
 
 
-def fetch(weights, held, sems):
-    for row_step in range(SIDE):
-        for lag in range(LAGS):
-            for b in range(SIDE):
-                tap = SIDE * (SIDE * lag + row_step) + b
-                pltpu.make_async_copy(weights.at[tap], held.at[tap], sems.at[tap]).start()
-
-
-def arrived(weights, held, sems, row_step):
-    for lag in range(LAGS):
-        for b in range(SIDE):
-            tap = SIDE * (SIDE * lag + row_step) + b
-            pltpu.make_async_copy(weights.at[tap], held.at[tap], sems.at[tap]).wait()
-
-
 def forward_body(parts, clips, where_ref, video, *refs):
     own, past = refs[:parts], refs[parts : 2 * parts]
-    weights, out, padded, acc, held, sems = refs[2 * parts :]
+    weights, out, padded, acc = refs[2 * parts :]
     frames, rows, width, chans = video.shape
     base, chan = where_ref[0], where_ref[1]
     lens = [where_ref[PLACES + i] for i in range(clips)]
-    fetch(weights, held, sems)
     edge = jnp.zeros((2 * frames, 1, width, chans), padded.dtype)
     for j in range(parts):
         shard = lax.rem(chan + j, parts)
@@ -90,25 +74,26 @@
         padded[shard, :, rows + 1 : rows + 2] = edge
         padded[shard, 0:frames, 1 : rows + 1] = past[j][...]
         padded[shard, frames : 2 * frames, 1 : rows + 1] = own[j][...]
-    acc[...] = jnp.zeros_like(acc)
 
     def step(row_step, carry):
-        arrived(weights, held, sems, row_step)
         taps = []
         for f in range(frames):
             frame = base + f
+            first = first_of(lens, clips, frame)
             pieces = []
             for lag in range(LAGS):
-                source = jnp.maximum(frame - lag, first_of(lens, clips, frame)) - base + frames
+                source = jnp.maximum(frame - lag, first) - base + frames
                 for j in range(parts):
                     pieces.append(padded[j, source, pl.ds(row_step, rows)].reshape(rows * width, chans))
             taps.append(jnp.concatenate(pieces, axis=1))
         taps = jnp.concatenate(taps, axis=0)
         for b in range(SIDE):
-            kernel = jnp.concatenate([held[SIDE * (SIDE * lag + row_step) + b] for lag in range(LAGS)], axis=0)
-            acc[b] += jnp.dot(taps, kernel, preferred_element_type=jnp.float32)
+            kernel = jnp.concatenate([weights[SIDE * (SIDE * lag + row_step) + b] for lag in range(LAGS)], axis=0)
+            terms = jnp.dot(taps, kernel, preferred_element_type=jnp.float32)
+            acc[b] += terms
         return carry
 
+    acc[...] = jnp.zeros_like(acc)
     lax.fori_loop(0, SIDE, step, 0)
     total = acc[1] + moved(acc[0], -1, width) + moved(acc[2], 1, width)
     out[...] = (video[...].astype(jnp.float32) + total.reshape(video.shape)).astype(out.dtype)
@@ -122,15 +107,13 @@
     return pl.pallas_call(
         functools.partial(forward_body, parts, where.shape[0] - PLACES),
         out_shape=jax.ShapeDtypeStruct(video.shape, video.dtype),
-        in_specs=[smem, whole] + [whole] * (2 * parts) + [pl.BlockSpec(memory_space=pltpu.HBM)],
+        in_specs=[smem, whole] + [whole] * (2 * parts) + [whole],
         out_specs=whole,
         scratch_shapes=[
             pltpu.VMEM((parts, 2 * frames, rows + 2, width, chans), video.dtype),
             pltpu.VMEM((SIDE, pixels, weights.shape[2]), jnp.float32),
-            pltpu.VMEM(weights.shape, weights.dtype),
-            pltpu.SemaphoreType.DMA((weights.shape[0],)),
         ],
-        compiler_params=pltpu.CompilerParams(vmem_limit_bytes=20 << 20),
+        compiler_params=pltpu.CompilerParams(vmem_limit_bytes=10 << 20),
         cost_estimate=pl.CostEstimate(
             flops=2 * pixels * weights.size, transcendentals=0, bytes_accessed=2 * weights.size),
         name="forward",
@@ -138,12 +121,11 @@
 
 
 def backward_body(parts, clips, where_ref, own, later, weights, mine, *refs):
-    others, (mixed, acc, held, sems) = refs[: parts - 1], refs[parts - 1 :]
+    others, (mixed, acc) = refs[: parts - 1], refs[parts - 1 :]
     frames, rows, width, chans = own.shape
     pixels = frames * rows * width
     base, chan = where_ref[0], where_ref[1]
     lens = [where_ref[PLACES + i] for i in range(clips)]
-    fetch(weights, held, sems)
     mixed[:, :, 0:1] = jnp.zeros((LAGS, frames, 1, width, chans), mixed.dtype)
     mixed[:, :, rows + 1 : rows + 2] = jnp.zeros((LAGS, frames, 1, width, chans), mixed.dtype)
     take = lambda f: (own[f] if f < frames else later[f - frames]).astype(jnp.float32)
@@ -157,17 +139,17 @@
         mixed[2, f, 1 : rows + 1] = (
             next_two * take(f + 2) + start * (take(f) + next_one * take(f + 1))
         ).astype(mixed.dtype)
-    acc[...] = jnp.zeros_like(acc)
 
     def step(row_step, carry):
-        arrived(weights, held, sems, row_step)
         taps = [mixed[lag, :, pl.ds(2 - row_step, rows)].reshape(pixels, chans) for lag in range(LAGS)]
         taps = jnp.concatenate(taps, axis=1)
         for b in range(SIDE):
-            kernel = jnp.concatenate([held[SIDE * (SIDE * lag + row_step) + b] for lag in range(LAGS)], axis=1)
-            acc[b] += lax.dot_general(taps, kernel, (((1,), (1,)), ((), ())), preferred_element_type=jnp.float32)
+            kernel = jnp.concatenate([weights[SIDE * (SIDE * lag + row_step) + b] for lag in range(LAGS)], axis=1)
+            terms = lax.dot_general(taps, kernel, (((1,), (1,)), ((), ())), preferred_element_type=jnp.float32)
+            acc[b] += terms
         return carry
 
+    acc[...] = jnp.zeros_like(acc)
     lax.fori_loop(0, SIDE, step, 0)
     for j in range(parts):
         at = pl.ds(pl.multiple_of(lax.rem(chan + j, parts) * chans, chans), chans)
@@ -187,15 +169,13 @@
         functools.partial(backward_body, parts, where.shape[0] - PLACES),
         out_shape=[jax.ShapeDtypeStruct(own.shape, jnp.float32)]
         + [jax.ShapeDtypeStruct(own.shape, own.dtype)] * (parts - 1),
-        in_specs=[smem, whole, whole, pl.BlockSpec(memory_space=pltpu.HBM)],
+        in_specs=[smem, whole, whole, whole],
         out_specs=[whole] * parts,
         scratch_shapes=[
             pltpu.VMEM((LAGS, frames, rows + 2, width, chans), own.dtype),
             pltpu.VMEM((SIDE, pixels, parts * chans), jnp.float32),
-            pltpu.VMEM(weights.shape, weights.dtype),
-            pltpu.SemaphoreType.DMA((weights.shape[0],)),
         ],
-        compiler_params=pltpu.CompilerParams(vmem_limit_bytes=20 << 20),
+        compiler_params=pltpu.CompilerParams(vmem_limit_bytes=10 << 20),
         cost_estimate=pl.CostEstimate(
             flops=2 * pixels * weights.size, transcendentals=0, bytes_accessed=2 * weights.size),
         name="backward",
@@ -203,7 +183,7 @@
 
 
 def turned_body(parts, where_ref, *refs):
-    own, outs, rows = refs[:parts], refs[parts:-1], refs[-1]
+    own, (*outs, rows) = refs[:parts], refs[parts:]
     chans = own[0].shape[1]
     for j in range(parts):
         shard = lax.rem(where_ref[1] + j, parts)
@@ -225,13 +205,14 @@
         out_specs=[whole] * pairs,
         scratch_shapes=[pltpu.VMEM((all_chans, pixels), own[0].dtype)],
         compiler_params=pltpu.CompilerParams(vmem_limit_bytes=4 << 20),
-        cost_estimate=pl.CostEstimate(flops=pixels * chans * 64, transcendentals=0, bytes_accessed=4 * pixels * chans),
+        cost_estimate=pl.CostEstimate(flops=4 << 30, transcendentals=0, bytes_accessed=4 * pixels * chans),
         name="turned",
     )(where, *own)
 
 
-def weight_body(blocks, group, rows, width, clips, scale, where_ref, *refs):
-    turned_refs, cots, (out, taps) = refs[:blocks], refs[blocks : 2 * blocks], refs[2 * blocks :]
+def weight_body(blocks, group, rows, width, clips, scale, where_ref, video, gain, mine, *refs):
+    turned_refs, cots = refs[:blocks], refs[blocks : 2 * blocks]
+    *others, out, input_grad, taps = refs[2 * blocks :]
     pixels = turned_refs[0].shape[1]
     area, chans, outs = rows * width, out.shape[3], out.shape[4]
     frames = pixels // area
@@ -260,6 +241,15 @@
                 sources = [jnp.maximum(frame - lag, first) for lag in range(LAGS)]
                 pieces.append(jnp.concatenate([taps[source] for source in sources], axis=0))
         pieces = jnp.concatenate(pieces, axis=1)
+        if start + group == blocks:
+            act_grad = mine[...]
+            for other in others:
+                act_grad = act_grad + other[...].astype(jnp.float32)
+            scaled = video[...].astype(jnp.float32) * gain[...]
+            sigmoid = 1.0 / (1.0 + jnp.exp(-scaled))
+            slope = sigmoid * (1.0 + scaled * (1.0 - sigmoid))
+            total = cots[0][...].astype(jnp.float32) + act_grad * slope * gain[...]
+            input_grad[...] = total.astype(input_grad.dtype)
         for row_step in range(SIDE):
             values = []
             for offset in offsets:
@@ -278,7 +268,7 @@
             out[:, row_step] = terms * scale if start + group == blocks else terms
 
 
-def weight_terms(where, turned_blocks, cots, rows, width, scale, group=2):
+def weight_terms(where, video, gain, mine, others, turned_blocks, cots, rows, width, scale, group=2):
     blocks, pixels = len(cots), cots[0].shape[0]
     chans = turned_blocks[0].shape[0] // 2
     outs = cots[0].shape[1]
@@ -286,18 +276,21 @@
     smem = pl.BlockSpec(memory_space=pltpu.SMEM)
     taps = LAGS * SIDE * SIDE
     frames = pixels // (rows * width)
-    result = pl.pallas_call(
+    result, input_grad = pl.pallas_call(
         functools.partial(weight_body, blocks, group, rows, width, where.shape[0] - PLACES, scale),
-        out_shape=jax.ShapeDtypeStruct((LAGS, SIDE, SIDE, chans, outs), jnp.float32),
-        in_specs=[smem] + [whole] * (2 * blocks),
-        out_specs=whole,
+        out_shape=[
+            jax.ShapeDtypeStruct((LAGS, SIDE, SIDE, chans, outs), jnp.float32),
+            jax.ShapeDtypeStruct(video.shape, video.dtype),
+        ],
+        in_specs=[smem] + [whole] * (3 + 2 * blocks + len(others)),
+        out_specs=[whole, whole],
         scratch_shapes=[pltpu.VMEM((blocks * frames, SIDE * chans, rows * width), turned_blocks[0].dtype)],
         compiler_params=pltpu.CompilerParams(vmem_limit_bytes=8 << 20),
         cost_estimate=pl.CostEstimate(
             flops=2 * blocks * pixels * taps * chans * outs, transcendentals=0, bytes_accessed=8 << 20),
         name="weight_terms",
-    )(where, *turned_blocks, *cots)
-    return result.reshape(taps, chans, outs)
+    )(where, video, gain.reshape(1, -1), mine, *turned_blocks, *cots, *others)
+    return result.reshape(taps, chans, outs), input_grad
 
 
 def extended_2(cells, sides, width):
@@ -492,9 +485,9 @@
     parts, shards = all_chans // chans, lax.axis_size("tm")
     pixels = frames * rows * width
     weights = pltpu.with_memory_space_constraint(weights, pltpu.HBM)
+    weights = pltpu.with_memory_space_constraint(weights, pltpu.VMEM)
     shard, chan = lax.axis_index("tm"), lax.axis_index("chan")
     where = jnp.concatenate([jnp.stack([shard * frames, chan, shard]), lengths]).astype(jnp.int32)
-    scaled = video.astype(jnp.float32) * channel_gain
     activated = silu(video.reshape(pixels, chans), channel_gain).reshape(video.shape)
     own = [activated] + [ahead(activated, "chan", j) for j in range(1, parts)]
     before = along(activated, "tm", 1)
@@ -502,21 +495,19 @@
     later = along(cotangent, "tm", -1)
     cots = gathered_blocks(cotangent.reshape(pixels, chans), "tm")
     mine, *others = backward(where, cotangent, later, weights)
-    act_grad = mine
-    for j in range(1, parts):
-        act_grad = act_grad + ahead(others[j - 1], "chan", parts - j).astype(jnp.float32)
+    others = [ahead(others[j - 1], "chan", parts - j).reshape(pixels, chans) for j in range(1, parts)]
     sent = turned(where, [x.reshape(pixels, chans) for x in own], shards // 2)
     blocks = []
     for offset in range(shards // 2):
         block = across(sent[offset], "tm", 2 * offset) if offset else sent[0]
         blocks += [block, across(block, "tm", 1)]
     output = forward(where, video, own, past, weights)
-    sigmoid_value = jax.nn.sigmoid(scaled)
-    slope_factor = sigmoid_value * (1.0 + scaled * (1.0 - sigmoid_value))
-    input_grad = (cotangent.astype(jnp.float32) + act_grad * slope_factor * channel_gain).astype(jnp.bfloat16)
     scale = 1.0 / math.sqrt(pixels * shards)
-    weight_grad = weight_terms(where, blocks, cots, rows, width, scale)
-    return (output, input_grad, weight_grad)
+    weight_grad, input_grad = weight_terms(
+        where, video.reshape(pixels, chans), channel_gain, mine.reshape(pixels, chans), others, blocks, cots,
+        rows, width, scale,
+    )
+    return (output, input_grad.reshape(video.shape), weight_grad)
 
 
 def solution(mesh):

time: 54.9 us -> 57.7 us (1.051)
  waiting for transfers between devices: 8.41 us -> 15.3 us
  Pallas kernels: 21.2 us -> 18.3 us
  other arithmetic: 1.74 us -> 0.73 us
  local copies, waits for them, and re-layouts: 2.59 us -> 1.65 us
  starting transfers between devices: 19.9 us -> 20.8 us
    ppermute x14, waiting for transfers between devices: 8.39 us -> 13.9 us  [across(): lax.ppermute(value, axis, [(i, i ^ offset) for i in range(lax.axis_size(a...]
    ppermute x14, starting transfers between devices: 12.1 us -> 13.9 us  [across(): lax.ppermute(value, axis, [(i, i ^ offset) for i in range(lax.axis_size(a...]
    pallas_call x1, Pallas kernels: 7.41 us -> 5.79 us  [forward(): pl.pallas_call(functools.partial(forward_body, parts, where.shape[0] - PL...]
    pallas_call x1, Pallas kernels: 6.89 us -> 5.54 us  [backward(): pl.pallas_call(functools.partial(backward_body, parts, where.shape[0] - P...]
    ppermute x3, waiting for transfers between devices: 0.01 us -> 1.34 us  [ahead(): lax.ppermute(value, axis, [((i + steps) % count, i) for i in range(count)])]
    convert_element_type x1 -> x0, other arithmetic: 1 us -> none  [whole_rows(): (cotangent.astype(jnp.float32) + act_grad * slope_factor * channel_gain)....]
    unnamed x10 -> x12, local copies, waits for them, and re-layouts: 2.59 us -> 1.65 us
    ppermute x3, starting transfers between devices: 5.06 us -> 4.17 us  [ahead(): lax.ppermute(value, axis, [((i + steps) % count, i) for i in range(count)])]
  transfers between devices with their start and end apart: 19 -> 19, of which waited for: 4 -> 5; matrix products, arithmetic and copies ran while one was open for 3% -> 1% of each run, Pallas kernels for 28% -> 21%
where the time goes in v2:
time: 57.7 us; the launch traced here: 57.5 us
  starting transfers between devices  20.8 us (36%)
  Pallas kernels  18.3 us (32%)
  waiting for transfers between devices  15.3 us (27%)
  local copies, waits for them, and re-layouts  1.65 us (3%)
  between operations  0.75 us (1%)
  other arithmetic  0.73 us (1%)
    ppermute x14, waiting for transfers between devices, across(): lax.ppermute(value, axis, [(i, i ^ offset) for i in range(lax.axis_size(a...  13.9 us
    ppermute x14, starting transfers between devices, across(): lax.ppermute(value, axis, [(i, i ^ offset) for i in range(lax.axis_size(a...  13.9 us
    pallas_call x1, Pallas kernels, weight_terms(): pl.pallas_call(functools.partial(weight_body, blocks, group, rows, width,...  6.09 us
    pallas_call x1, Pallas kernels, forward(): pl.pallas_call(functools.partial(forward_body, parts, where.shape[0] - PL...  5.79 us
    pallas_call x1, Pallas kernels, backward(): pl.pallas_call(functools.partial(backward_body, parts, where.shape[0] - P...  5.54 us
    ppermute x3, starting transfers between devices, ahead(): lax.ppermute(value, axis, [((i + steps) % count, i) for i in range(count)])  4.17 us
    ppermute x2, starting transfers between devices, along(): lax.ppermute(value, axis, [(source, source + steps) for source in range(f...  2.75 us
    unnamed x12, local copies, waits for them, and re-layouts  1.65 us
  transfers between devices with their start and end apart: 19, of which 5 were waited for; matrix products, arithmetic and copies ran while one was open for 1% of the time, Pallas kernels for 21%

profile of v2, /device:TPU:0, one launch (start us, length us, event | category | flops | bytes accessed | tf_op | source)
XLA Modules:
  0.0 57.5 jit_solution(4137407509093364422)
XLA Ops:
  0.6 0.0 copy-start
  0.6 0.9 %copy-done = bf16[2,8,32,256]{3,2,1,0:T(8,128)(2,1)S(1)} copy-done((bf16[2,8,32,256]{3,2,1,0:T(8,128)(2,1)S(1)}, bf16[2,8,32,256]{3,2,1,0:T(8,128)(2,1)}, u32[]{:S(2)}) %copy-start) | copy-done | bytes 262168
  1.6 0.7 %copy-done.2 = f32[256]{0:T(256)S(1)} copy-done((f32[256]{0:T(256)S(1)}, f32[256]{0:T(256)}, u32[]{:S(2)}) %copy-start.2) | copy-done | bytes 1048
  2.3 0.2 silu.1.refs_0_
  2.4 3.0 %collective-permute-start = (bf16[2,8,32,256]{3,2,1,0:T(8,128)(2,1)S(1)}, bf16[2,8,32,256]{3,2,1,0:T(8,128)(2,1)S(1)}, u32[]{:S(2)}, u32[]{:S(2)}) collective-permute-start(bf16[2,8,32,256]{3,2,1,0:T(8,128)(2,1)S(1)} %bitcast.14), channel_id=1, source_target_pairs={{1,0},{0,1},{3,2},{2,3},{5,4},{4,5},{7,6},{6,7},{9,8},{8,9},{11,10... | collective-permute-start | bytes 786440 | tf_op jit(solution)/shard_map/ppermute | solution.py:469
  5.5 1.5 %collective-permute-start.1 = (bf16[2,8,32,256]{3,2,1,0:T(8,128)(2,1)S(1)}, bf16[2,8,32,256]{3,2,1,0:T(8,128)(2,1)S(1)}, u32[]{:S(2)}, u32[]{:S(2)}) collective-permute-start(bf16[2,8,32,256]{3,2,1,0:T(8,128)(2,1)S(1)} %bitcast.15), channel_id=1, source_target_pairs={{0,2},{2,4},{4,6},{6,8},{8,10},{10,12},{12,14},{1,3},{3,5},{5,7},{... | collective-permute-start | bytes 786440 | tf_op jit(solution)/shard_map/ppermute | solution.py:460
  6.9 3.1 %collective-permute-start.14 = (bf16[512,256]{1,0:T(8,128)(2,1)}, bf16[512,256]{1,0:T(8,128)(2,1)S(1)}, u32[]{:S(2)}, u32[]{:S(2)}) collective-permute-start(bf16[512,256]{1,0:T(8,128)(2,1)} %bitcast.19), channel_id=1, source_target_pairs={{0,8},{2,10},{4,12},{6,14},{8,0},{10,2},{12,4},{14,6},{1,9},{3,11}... | collective-permute-start | bytes 786440 | tf_op jit(solution)/shard_map/ppermute | solution.py:464
  10.0 1.6 %collective-permute-start.12 = (bf16[512,256]{1,0:T(8,128)(2,1)}, bf16[512,256]{1,0:T(8,128)(2,1)S(1)}, u32[]{:S(2)}, u32[]{:S(2)}) collective-permute-start(bf16[512,256]{1,0:T(8,128)(2,1)} %bitcast.20), channel_id=1, source_target_pairs={{0,4},{2,6},{4,0},{6,2},{8,12},{10,14},{12,8},{14,10},{1,5},{3,7},... | collective-permute-start | bytes 786440 | tf_op jit(solution)/shard_map/ppermute | solution.py:464
  11.6 0.0 collective-permute-start.11
  11.6 0.7 %pad_add_fusion.where_ref = s32[7]{0:T(128)S(1)} fusion(s32[4]{0:T(128)} %param.8, s32[1]{0:T(128)} %bitcast.2, s32[1]{0:T(128)} %bitcast.1, s32[1]{0:T(128)} %bitcast), kind=kLoop, calls=%fused_computation | loop fusion | flops 21 | bytes 56 | tf_op jit(solution)/shard_map/concatenate | solution.py:490
  12.3 0.0 collective-permute-done.refs_1_
  12.3 1.3 %collective-permute-start.3 = (bf16[2,8,32,256]{3,2,1,0:T(8,128)(2,1)}, bf16[2,8,32,256]{3,2,1,0:T(8,128)(2,1)S(1)}, u32[]{:S(2)}, u32[]{:S(2)}) collective-permute-start(bf16[2,8,32,256]{3,2,1,0:T(8,128)(2,1)} %own.1), channel_id=1, source_target_pairs={{2,0},{4,2},{6,4},{8,6},{10,8},{12,10},{14,12},{3,1},{5,3},{7,5},{... | collective-permute-start | bytes 786440 | tf_op jit(solution)/shard_map/ppermute | solution.py:460
  13.6 0.0 copy-start.4
  13.6 0.0 copy-start.5
  13.7 0.8 %turned.1 = (bf16[128,512]{1,0:T(8,128)(2,1)S(1)}, bf16[128,512]{1,0:T(8,128)(2,1)S(1)}, bf16[128,512]{1,0:T(8,128)(2,1)S(1)}, bf16[128,512]{1,0:T(8,128)(2,1)S(1)}) custom-call(s32[7]{0:T(128)S(1)} %pad_add_fusion.where_ref, bf16[512,256]{1,0:T(8,128)(2,1)S(1)} %silu.1.refs_0_, bf16[512,256]{1,0:T(8,128)(2,1)S(1)} %bitcast.23), custom_call_target="tpu_custom_call" | custom-call | flops 4294967296 | bytes 524288 | tf_op jit(solution)/shard_map/turned/pallas_call | solution.py:201
  14.4 0.0 copy-start.1
  14.4 2.8 %collective-permute-start.5 = (bf16[128,512]{1,0:T(8,128)(2,1)S(1)}, bf16[128,512]{1,0:T(8,128)(2,1)S(1)}, u32[]{:S(2)}, u32[]{:S(2)}) collective-permute-start(bf16[128,512]{1,0:T(8,128)(2,1)S(1)} %get-tuple-element.13), channel_id=1, source_target_pairs={{0,4},{2,6},{4,0},{6,2},{8,12},{10,14},{12,8},{14,10},{1,5},{3,7},... | collective-permute-start | bytes 393224 | tf_op jit(solution)/shard_map/ppermute | solution.py:464
  17.3 4.8 %collective-permute-done.14.refs_12_ = bf16[512,256]{1,0:T(8,128)(2,1)S(1)} collective-permute-done((bf16[512,256]{1,0:T(8,128)(2,1)}, bf16[512,256]{1,0:T(8,128)(2,1)S(1)}, u32[]{:S(2)}, u32[]{:S(2)}) %collective-permute-start.14) | collective-permute-done | bytes 262176 | tf_op jit(solution)/shard_map/ppermute | solution.py:464
  22.1 0.2 collective-permute-start.7
  22.3 0.4 collective-permute-done.12.refs_10_
  22.7 4.3 %collective-permute-start.9 = (bf16[128,512]{1,0:T(8,128)(2,1)S(1)}, bf16[128,512]{1,0:T(8,128)(2,1)S(1)}, u32[]{:S(2)}, u32[]{:S(2)}) collective-permute-start(bf16[128,512]{1,0:T(8,128)(2,1)S(1)} %get-tuple-element.15), channel_id=1, source_target_pairs={{0,12},{2,14},{4,8},{6,10},{8,4},{10,6},{12,0},{14,2},{1,13},{3,15... | collective-permute-start | bytes 393224 | tf_op jit(solution)/shard_map/ppermute | solution.py:464
  27.0 0.0 collective-permute-done.11.refs_9_
  27.0 0.8 %collective-permute-start.4 = (bf16[128,512]{1,0:T(8,128)(2,1)S(1)}, bf16[128,512]{1,0:T(8,128)(2,1)S(1)}, u32[]{:S(2)}, u32[]{:S(2)}) collective-permute-start(bf16[128,512]{1,0:T(8,128)(2,1)S(1)} %get-tuple-element.12.refs_0_), channel_id=1, source_target_pairs={{0,2},{2,0},{4,6},{6,4},{8,10},{10,8},{12,14},{14,12},{1,3},{3,1},... | collective-permute-start | bytes 393224 | tf_op jit(solution)/shard_map/ppermute | solution.py:464
  27.8 0.5 collective-permute-start.2
  28.4 4.1 %collective-permute-done.5.refs_2_ = bf16[128,512]{1,0:T(8,128)(2,1)S(1)} collective-permute-done((bf16[128,512]{1,0:T(8,128)(2,1)S(1)}, bf16[128,512]{1,0:T(8,128)(2,1)S(1)}, u32[]{:S(2)}, u32[]{:S(2)}) %collective-permute-start.5) | collective-permute-done | bytes 131104 | tf_op jit(solution)/shard_map/ppermute | solution.py:464
  32.5 0.0 collective-permute-start.16
  32.5 0.0 collective-permute-done.7.refs_4_
  32.5 0.0 collective-permute-start.6
  32.5 4.6 %collective-permute-done.9.refs_6_ = bf16[128,512]{1,0:T(8,128)(2,1)S(1)} collective-permute-done((bf16[128,512]{1,0:T(8,128)(2,1)S(1)}, bf16[128,512]{1,0:T(8,128)(2,1)S(1)}, u32[]{:S(2)}, u32[]{:S(2)}) %collective-permute-start.9) | collective-permute-done | bytes 131104 | tf_op jit(solution)/shard_map/ppermute | solution.py:464
  37.1 5.5 %backward.1 = (f32[2,8,32,256]{3,2,1,0:T(8,128)S(1)}, bf16[2,8,32,256]{3,2,1,0:T(8,128)(2,1)S(1)}) custom-call(s32[7]{0:T(128)S(1)} %pad_add_fusion.where_ref, bf16[2,8,32,256]{3,2,1,0:T(8,128)(2,1)S(1)} %copy-done.5, bf16[2,8,32,256]{3,2,1,0:T(8,128)(2,1)S(1)} %collective-permute-done.3.later, bf16[27,512,256]{2,1,0:T(8,128)(2,1)S(1)} %copy-done.4), custom_call_target="tpu_custom_call" | custom-call | flops 3623878656 | bytes 7077888 | tf_op jit(solution)/shard_map/backward/pallas_call | solution.py:168
  42.6 0.0 copy-start.3
  42.6 0.0 collective-permute-done.4.refs_1_
  42.7 0.6 %collective-permute-start.18 = (bf16[2,8,32,256]{3,2,1,0:T(8,128)(2,1)S(1)}, bf16[2,8,32,256]{3,2,1,0:T(8,128)(2,1)S(1)}, u32[]{:S(2)}, u32[]{:S(2)}) collective-permute-start(bf16[2,8,32,256]{3,2,1,0:T(8,128)(2,1)S(1)} %get-tuple-element.16), channel_id=1, source_target_pairs={{1,0},{0,1},{3,2},{2,3},{5,4},{4,5},{7,6},{6,7},{9,8},{8,9},{11,10... | collective-permute-start | bytes 786440 | tf_op jit(solution)/shard_map/ppermute | solution.py:469
  43.3 0.0 collective-permute-done.2.refs_3_
  43.3 0.2 collective-permute-start.15
  43.5 0.0 collective-permute-done.6.refs_3_
  43.5 0.3 collective-permute-start.13
  43.8 0.0 collective-permute-done.8.refs_5_
  43.8 0.2 collective-permute-start.10
  44.0 0.0 collective-permute-done.16.refs_14_
  44.0 0.3 collective-permute-start.17
  44.3 5.8 %forward.1 = bf16[2,8,32,256]{3,2,1,0:T(8,128)(2,1)} custom-call(s32[7]{0:T(128)S(1)} %pad_add_fusion.where_ref, bf16[2,8,32,256]{3,2,1,0:T(8,128)(2,1)S(1)} %copy-done.1, bf16[2,8,32,256]{3,2,1,0:T(8,128)(2,1)S(1)} %bitcast.16, bf16[2,8,32,256]{3,2,1,0:T(8,128)(2,1)S(1)} %collective-permute-done.refs_1_, ...), custom_call_target="tpu_custom_call" | custom-call | flops 3623878656 | bytes 7077888 | tf_op jit(solution)/shard_map/forward/pallas_call | solution.py:107
  50.1 0.0 collective-permute-done.10.refs_7_
  50.1 0.0 collective-permute-done.15.refs_13_
  50.1 0.0 collective-permute-done.13.refs_11_
  50.1 1.3 %collective-permute-done.18 = bf16[2,8,32,256]{3,2,1,0:T(8,128)(2,1)S(1)} collective-permute-done((bf16[2,8,32,256]{3,2,1,0:T(8,128)(2,1)S(1)}, bf16[2,8,32,256]{3,2,1,0:T(8,128)(2,1)S(1)}, u32[]{:S(2)}, u32[]{:S(2)}) %collective-permute-start.18) | collective-permute-done | bytes 262176 | tf_op jit(solution)/shard_map/ppermute | solution.py:469
  51.4 0.0 collective-permute-done.17.refs_15_
  51.4 6.1 %weight_terms.1 = (f32[3,3,3,64,256]{4,3,2,1,0:T(8,128)}, bf16[512,256]{1,0:T(8,128)(2,1)}) custom-call(s32[7]{0:T(128)S(1)} %pad_add_fusion.where_ref, bf16[512,256]{1,0:T(8,128)(2,1)S(1)} %bitcast.13, f32[1,256]{1,0:T(1,128)S(1)} %bitcast.18, f32[512,256]{1,0:T(8,128)S(1)} %bitcast.25, bf16[128,512]{1,0:T(8,128)(2,1)S(1)} %get-tuple-element.12.refs_0_, ...), custom_call_target="tpu_custom_call" | custom-call | flops 3623878656 | bytes 8388608 | tf_op jit(solution)/shard_map/weight_terms/pallas_call | solution.py:279
  (8 shorter events, 0.0 us)
Async XLA Ops:
  0.6 1.0 %copy-start = (bf16[2,8,32,256]{3,2,1,0:T(8,128)(2,1)S(1)}, bf16[2,8,32,256]{3,2,1,0:T(8,128)(2,1)}, u32[]{:S(2)}) copy-start(bf16[2,8,32,256]{3,2,1,0:T(8,128)(2,1)} %video.1) | copy-start | bytes 786436
  1.6 0.7 %copy-start.2 = (f32[256]{0:T(256)S(1)}, f32[256]{0:T(256)}, u32[]{:S(2)}) copy-start(f32[256]{0:T(256)} %param.6) | copy-start | bytes 3076
  2.4 9.9 %collective-permute-start = (bf16[2,8,32,256]{3,2,1,0:T(8,128)(2,1)S(1)}, bf16[2,8,32,256]{3,2,1,0:T(8,128)(2,1)S(1)}, u32[]{:S(2)}, u32[]{:S(2)}) collective-permute-start(bf16[2,8,32,256]{3,2,1,0:T(8,128)(2,1)S(1)} %bitcast.14), channel_id=1, source_target_pairs={{1,0},{0,1},{3,2},{2,3},{5,4},{4,5},{7,6},{6,7},{9,8},{8,9},{11,10... | collective-permute-start | bytes 786440 | tf_op jit(solution)/shard_map/ppermute | solution.py:469
  5.5 9.0 %collective-permute-start.1 = (bf16[2,8,32,256]{3,2,1,0:T(8,128)(2,1)S(1)}, bf16[2,8,32,256]{3,2,1,0:T(8,128)(2,1)S(1)}, u32[]{:S(2)}, u32[]{:S(2)}) collective-permute-start(bf16[2,8,32,256]{3,2,1,0:T(8,128)(2,1)S(1)} %bitcast.15), channel_id=1, source_target_pairs={{0,2},{2,4},{4,6},{6,8},{8,10},{10,12},{12,14},{1,3},{3,5},{5,7},{... | collective-permute-start | bytes 786440 | tf_op jit(solution)/shard_map/ppermute | solution.py:460
  6.9 15.2 %collective-permute-start.14 = (bf16[512,256]{1,0:T(8,128)(2,1)}, bf16[512,256]{1,0:T(8,128)(2,1)S(1)}, u32[]{:S(2)}, u32[]{:S(2)}) collective-permute-start(bf16[512,256]{1,0:T(8,128)(2,1)} %bitcast.19), channel_id=1, source_target_pairs={{0,8},{2,10},{4,12},{6,14},{8,0},{10,2},{12,4},{14,6},{1,9},{3,11}... | collective-permute-start | bytes 786440 | tf_op jit(solution)/shard_map/ppermute | solution.py:464
  10.0 12.7 %collective-permute-start.12 = (bf16[512,256]{1,0:T(8,128)(2,1)}, bf16[512,256]{1,0:T(8,128)(2,1)S(1)}, u32[]{:S(2)}, u32[]{:S(2)}) collective-permute-start(bf16[512,256]{1,0:T(8,128)(2,1)} %bitcast.20), channel_id=1, source_target_pairs={{0,4},{2,6},{4,0},{6,2},{8,12},{10,14},{12,8},{14,10},{1,5},{3,7},... | collective-permute-start | bytes 786440 | tf_op jit(solution)/shard_map/ppermute | solution.py:464
  11.6 15.4 %collective-permute-start.11 = (bf16[512,256]{1,0:T(8,128)(2,1)}, bf16[512,256]{1,0:T(8,128)(2,1)S(1)}, u32[]{:S(2)}, u32[]{:S(2)}) collective-permute-start(bf16[512,256]{1,0:T(8,128)(2,1)} %bitcast.21), channel_id=1, source_target_pairs={{0,2},{2,0},{4,6},{6,4},{8,10},{10,8},{12,14},{14,12},{1,3},{3,1},... | collective-permute-start | bytes 786440 | tf_op jit(solution)/shard_map/ppermute | solution.py:464
  12.3 15.5 %collective-permute-start.3 = (bf16[2,8,32,256]{3,2,1,0:T(8,128)(2,1)}, bf16[2,8,32,256]{3,2,1,0:T(8,128)(2,1)S(1)}, u32[]{:S(2)}, u32[]{:S(2)}) collective-permute-start(bf16[2,8,32,256]{3,2,1,0:T(8,128)(2,1)} %own.1), channel_id=1, source_target_pairs={{2,0},{4,2},{6,4},{8,6},{10,8},{12,10},{14,12},{3,1},{5,3},{7,5},{... | collective-permute-start | bytes 786440 | tf_op jit(solution)/shard_map/ppermute | solution.py:460
  13.6 23.5 %copy-start.4 = (bf16[27,512,256]{2,1,0:T(8,128)(2,1)S(1)}, bf16[27,512,256]{2,1,0:T(8,128)(2,1)}, u32[]{:S(2)}) copy-start(bf16[27,512,256]{2,1,0:T(8,128)(2,1)} %weights.1) | copy-start | bytes 21233668
  13.6 23.4 %copy-start.5 = (bf16[2,8,32,256]{3,2,1,0:T(8,128)(2,1)S(1)}, bf16[2,8,32,256]{3,2,1,0:T(8,128)(2,1)}, u32[]{:S(2)}) copy-start(bf16[2,8,32,256]{3,2,1,0:T(8,128)(2,1)} %own.1) | copy-start | bytes 786436
  14.4 29.9 %copy-start.1 = (bf16[2,8,32,256]{3,2,1,0:T(8,128)(2,1)S(1)}, bf16[2,8,32,256]{3,2,1,0:T(8,128)(2,1)}, u32[]{:S(2)}) copy-start(bf16[2,8,32,256]{3,2,1,0:T(8,128)(2,1)} %video.1) | copy-start | bytes 786436
  14.4 18.0 %collective-permute-start.5 = (bf16[128,512]{1,0:T(8,128)(2,1)S(1)}, bf16[128,512]{1,0:T(8,128)(2,1)S(1)}, u32[]{:S(2)}, u32[]{:S(2)}) collective-permute-start(bf16[128,512]{1,0:T(8,128)(2,1)S(1)} %get-tuple-element.13), channel_id=1, source_target_pairs={{0,4},{2,6},{4,0},{6,2},{8,12},{10,14},{12,8},{14,10},{1,5},{3,7},... | collective-permute-start | bytes 393224 | tf_op jit(solution)/shard_map/ppermute | solution.py:464
  22.1 10.4 %collective-permute-start.7 = (bf16[128,512]{1,0:T(8,128)(2,1)S(1)}, bf16[128,512]{1,0:T(8,128)(2,1)S(1)}, u32[]{:S(2)}, u32[]{:S(2)}) collective-permute-start(bf16[128,512]{1,0:T(8,128)(2,1)S(1)} %get-tuple-element.14), channel_id=1, source_target_pairs={{0,8},{2,10},{4,12},{6,14},{8,0},{10,2},{12,4},{14,6},{1,9},{3,11}... | collective-permute-start | bytes 393224 | tf_op jit(solution)/shard_map/ppermute | solution.py:464
  22.7 14.4 %collective-permute-start.9 = (bf16[128,512]{1,0:T(8,128)(2,1)S(1)}, bf16[128,512]{1,0:T(8,128)(2,1)S(1)}, u32[]{:S(2)}, u32[]{:S(2)}) collective-permute-start(bf16[128,512]{1,0:T(8,128)(2,1)S(1)} %get-tuple-element.15), channel_id=1, source_target_pairs={{0,12},{2,14},{4,8},{6,10},{8,4},{10,6},{12,0},{14,2},{1,13},{3,15... | collective-permute-start | bytes 393224 | tf_op jit(solution)/shard_map/ppermute | solution.py:464
  27.0 15.6 %collective-permute-start.4 = (bf16[128,512]{1,0:T(8,128)(2,1)S(1)}, bf16[128,512]{1,0:T(8,128)(2,1)S(1)}, u32[]{:S(2)}, u32[]{:S(2)}) collective-permute-start(bf16[128,512]{1,0:T(8,128)(2,1)S(1)} %get-tuple-element.12.refs_0_), channel_id=1, source_target_pairs={{0,2},{2,0},{4,6},{6,4},{8,10},{10,8},{12,14},{14,12},{1,3},{3,1},... | collective-permute-start | bytes 393224 | tf_op jit(solution)/shard_map/ppermute | solution.py:464
  27.8 15.4 %collective-permute-start.2 = (bf16[2,8,32,256]{3,2,1,0:T(8,128)(2,1)S(1)}, bf16[2,8,32,256]{3,2,1,0:T(8,128)(2,1)S(1)}, u32[]{:S(2)}, u32[]{:S(2)}) collective-permute-start(bf16[2,8,32,256]{3,2,1,0:T(8,128)(2,1)S(1)} %collective-permute-done.1.refs_2_), channel_id=1, source_target_pairs={{1,0},{0,1},{3,2},{2,3},{5,4},{4,5},{7,6},{6,7},{9,8},{8,9},{11,10... | collective-permute-start | bytes 786440 | tf_op jit(solution)/shard_map/ppermute | solution.py:469
  32.5 11.5 %collective-permute-start.16 = (bf16[512,256]{1,0:T(8,128)(2,1)S(1)}, bf16[512,256]{1,0:T(8,128)(2,1)S(1)}, u32[]{:S(2)}, u32[]{:S(2)}) collective-permute-start(bf16[512,256]{1,0:T(8,128)(2,1)S(1)} %collective-permute-done.14.refs_12_), channel_id=1, source_target_pairs={{0,4},{2,6},{4,0},{6,2},{8,12},{10,14},{12,8},{14,10},{1,5},{3,7},... | collective-permute-start | bytes 786440 | tf_op jit(solution)/shard_map/ppermute | solution.py:464
  32.5 11.0 %collective-permute-start.6 = (bf16[128,512]{1,0:T(8,128)(2,1)S(1)}, bf16[128,512]{1,0:T(8,128)(2,1)S(1)}, u32[]{:S(2)}, u32[]{:S(2)}) collective-permute-start(bf16[128,512]{1,0:T(8,128)(2,1)S(1)} %collective-permute-done.5.refs_2_), channel_id=1, source_target_pairs={{0,2},{2,0},{4,6},{6,4},{8,10},{10,8},{12,14},{14,12},{1,3},{3,1},... | collective-permute-start | bytes 393224 | tf_op jit(solution)/shard_map/ppermute | solution.py:464
  37.1 6.7 %collective-permute-start.8 = (bf16[128,512]{1,0:T(8,128)(2,1)S(1)}, bf16[128,512]{1,0:T(8,128)(2,1)S(1)}, u32[]{:S(2)}, u32[]{:S(2)}) collective-permute-start(bf16[128,512]{1,0:T(8,128)(2,1)S(1)} %collective-permute-done.7.refs_4_), channel_id=1, source_target_pairs={{0,2},{2,0},{4,6},{6,4},{8,10},{10,8},{12,14},{14,12},{1,3},{3,1},... | collective-permute-start | bytes 393224 | tf_op jit(solution)/shard_map/ppermute | solution.py:464
  42.6 8.8 %copy-start.3 = (f32[256]{0:T(256)S(1)}, f32[256]{0:T(256)}, u32[]{:S(2)}) copy-start(f32[256]{0:T(256)} %param.6) | copy-start | bytes 3076
  42.7 8.8 %collective-permute-start.18 = (bf16[2,8,32,256]{3,2,1,0:T(8,128)(2,1)S(1)}, bf16[2,8,32,256]{3,2,1,0:T(8,128)(2,1)S(1)}, u32[]{:S(2)}, u32[]{:S(2)}) collective-permute-start(bf16[2,8,32,256]{3,2,1,0:T(8,128)(2,1)S(1)} %get-tuple-element.16), channel_id=1, source_target_pairs={{1,0},{0,1},{3,2},{2,3},{5,4},{4,5},{7,6},{6,7},{9,8},{8,9},{11,10... | collective-permute-start | bytes 786440 | tf_op jit(solution)/shard_map/ppermute | solution.py:469
  43.3 6.8 %collective-permute-start.15 = (bf16[512,256]{1,0:T(8,128)(2,1)S(1)}, bf16[512,256]{1,0:T(8,128)(2,1)S(1)}, u32[]{:S(2)}, u32[]{:S(2)}) collective-permute-start(bf16[512,256]{1,0:T(8,128)(2,1)S(1)} %collective-permute-done.14.refs_12_), channel_id=1, source_target_pairs={{0,2},{2,0},{4,6},{6,4},{8,10},{10,8},{12,14},{14,12},{1,3},{3,1},... | collective-permute-start | bytes 786440 | tf_op jit(solution)/shard_map/ppermute | solution.py:464
  43.5 6.6 %collective-permute-start.13 = (bf16[512,256]{1,0:T(8,128)(2,1)S(1)}, bf16[512,256]{1,0:T(8,128)(2,1)S(1)}, u32[]{:S(2)}, u32[]{:S(2)}) collective-permute-start(bf16[512,256]{1,0:T(8,128)(2,1)S(1)} %collective-permute-done.12.refs_10_), channel_id=1, source_target_pairs={{0,2},{2,0},{4,6},{6,4},{8,10},{10,8},{12,14},{14,12},{1,3},{3,1},... | collective-permute-start | bytes 786440 | tf_op jit(solution)/shard_map/ppermute | solution.py:464
  43.8 6.3 %collective-permute-start.10 = (bf16[128,512]{1,0:T(8,128)(2,1)S(1)}, bf16[128,512]{1,0:T(8,128)(2,1)S(1)}, u32[]{:S(2)}, u32[]{:S(2)}) collective-permute-start(bf16[128,512]{1,0:T(8,128)(2,1)S(1)} %collective-permute-done.9.refs_6_), channel_id=1, source_target_pairs={{0,2},{2,0},{4,6},{6,4},{8,10},{10,8},{12,14},{14,12},{1,3},{3,1},... | collective-permute-start | bytes 393224 | tf_op jit(solution)/shard_map/ppermute | solution.py:464
  44.0 7.4 %collective-permute-start.17 = (bf16[512,256]{1,0:T(8,128)(2,1)S(1)}, bf16[512,256]{1,0:T(8,128)(2,1)S(1)}, u32[]{:S(2)}, u32[]{:S(2)}) collective-permute-start(bf16[512,256]{1,0:T(8,128)(2,1)S(1)} %collective-permute-done.16.refs_14_), channel_id=1, source_target_pairs={{0,2},{2,0},{4,6},{6,4},{8,10},{10,8},{12,14},{14,12},{1,3},{3,1},... | collective-permute-start | bytes 786440 | tf_op jit(solution)/shard_map/ppermute | solution.py:464
